TPU v7x, 32 devices: a whole 2x2x4 slice. The times are simulated.
32 devices in a mesh: query: 8 (over z, y), cand: 4 (over x, core).
Axes of the slice: x: 2, y: 2, z: 4, core: 2. Of those that a mesh axis runs over, the one named last changes fastest.
Arguments:
- tokens: bfloat16 [2, 8, 4, 512, 768], P(None, 'query', 'cand'), may hold values from -6 to 6
- cotangent: bfloat16 [2, 8, 4, 512, 768], P(None, 'query', 'cand'), may hold values from -6 to 6
- lengths: int32 [2, 8, 4, 2], P(None, 'query'), may hold values from 0 to 512, as said below
- relevance: float32 [2, 8, 4, 2], P(None, 'query'), may hold values from -8 to 8
- rel_table: int32 [1023], replicated, may hold values from 0 to 255
- w_query: bfloat16 [768, 768], P('query'), may hold values from -0.21875 to 0.21875
- w_key: bfloat16 [768, 768], P('query'), may hold values from -0.21875 to 0.21875
- w_value: bfloat16 [768, 768], P('query'), may hold values from -0.21875 to 0.21875
- w_output: bfloat16 [768, 768], P('query'), may hold values from -3.5 to 3.5
- w_inner: bfloat16 [768, 3072], P('query'), may hold values from -0.21875 to 0.21875
- w_outer: bfloat16 [3072, 768], P('query'), may hold values from -0.109375 to 0.109375
- bias_query: bfloat16 [768], P('query'), may hold values from -3 to 3
- bias_value: bfloat16 [768], P('query'), may hold values from -3 to 3
- bias_attn: bfloat16 [768], P('query'), may hold values from -3 to 3
- bias_inner: bfloat16 [3072], P('query'), may hold values from -3 to 3
- bias_outer: bfloat16 [768], P('query'), may hold values from -3 to 3
- gain_attn: bfloat16 [768], P('query'), may hold values from 0.099609375 to 1.8984375
- shift_attn: bfloat16 [768], P('query'), may hold values from -3 to 3
- gain_ffn: bfloat16 [768], P('query'), may hold values from 0.099609375 to 1.8984375
- shift_ffn: bfloat16 [768], P('query'), may hold values from -3 to 3
- rel_bias: bfloat16 [256, 12], P('query'), may hold values from -5 to 5
- w_score: bfloat16 [768], P('query'), may hold values from -0.3125 to 0.3125
Outputs:
- hidden: bfloat16 [2, 8, 4, 512, 768], P(None, 'query', 'cand')
- query_loss: float32 [2, 8], P(None, 'query')
- grad_tokens: float32 [2, 8, 4, 512, 768], P(None, 'query', 'cand')
- grad_w_query: float32 [768, 768], P(('query', 'cand'))
- grad_w_key: float32 [768, 768], P(('query', 'cand'))
- grad_w_value: float32 [768, 768], P(('query', 'cand'))
- grad_w_output: float32 [768, 768], P(('query', 'cand'))
- grad_w_inner: float32 [768, 3072], P(('query', 'cand'))
- grad_w_outer: float32 [3072, 768], P(('query', 'cand'))
- grad_bias_query: float32 [768], P(('query', 'cand'))
- grad_bias_value: float32 [768], P(('query', 'cand'))
- grad_bias_attn: float32 [768], P(('query', 'cand'))
- grad_bias_inner: float32 [3072], P(('query', 'cand'))
- grad_bias_outer: float32 [768], P(('query', 'cand'))
- grad_gain_attn: float32 [768], P(('query', 'cand'))
- grad_shift_attn: float32 [768], P(('query', 'cand'))
- grad_gain_ffn: float32 [768], P(('query', 'cand'))
- grad_shift_ffn: float32 [768], P(('query', 'cand'))
- grad_rel_bias: float32 [256, 12], P(('query', 'cand'))
- grad_w_score: float32 [768], P(('query', 'cand'))
Inputs may be any that keep to these rules, and one draw needn't show every extreme that they name: `lengths`: A slot holds one sequence of 256 to 512 tokens (second length 0) or two of 128 to 256 tokens each; some slot holds one of exactly 512 tokens and some two of exactly 256.
All inputs are finite; a program needn't handle non-finite values.
Results may differ from a plain program's by a relative error of at most 0.017.
Values may be sent and summed in bfloat16 or wider, within the bound.
No kernel may reach another device: no remote copies, remote signals or barrier semaphores. Data moves between devices by JAX's collectives and lax.ppermute only.
A program may use at most 192 MiB of HBM per device.

v0:
```python
from functools import partial

import jax
import jax.numpy as jnp
import numpy as np
from jax import lax
from jax.experimental import pallas as pl
from jax.experimental.pallas import tpu as pltpu
from jax.sharding import PartitionSpec as P

HD = 64
PAIR = 2 * HD
TRIO = 3 * PAIR
TILE = 128
BF = jnp.bfloat16
F32 = jnp.float32
NEG = -1000000000.0
EPS = 1e-05

ERFC_P = 0.3
ERFC_C = (
    0.16919777981386785,
    0.17054619772689322,
    0.14956727662616615,
    0.21002273459109255,
    -0.08286335340540726,
    0.5302129644860679,
    -0.49655482906135956,
    0.4777385344298923,
    -0.12786727948795917,
)

VECTORS = (
    "bias_query",
    "bias_value",
    "bias_attn",
    "bias_outer",
    "gain_attn",
    "shift_attn",
    "gain_ffn",
    "shift_ffn",
    "w_score",
)
TABLE_ROWS = 16
ROW = {name: index for index, name in enumerate(VECTORS)}


def cost(micros=0.001):
    return pl.CostEstimate(flops=int(micros * 1.15e9), bytes_accessed=0, transcendentals=0)


def contract(left_mat, right_mat, left_dim, right_dim):
    return lax.dot_general(
        left_mat,
        right_mat,
        (((left_dim,), (right_dim,)), ((), ())),
        preferred_element_type=F32,
    )


def gelu_pair(u):
    size = jnp.abs(u)
    t = 1.0 / (1.0 + (ERFC_P * 0.5**0.5) * size)
    poly = jnp.full_like(u, 0.5 * ERFC_C[-1])
    for coef in ERFC_C[-2::-1]:
        poly = poly * t + 0.5 * coef
    bell = jnp.exp(-0.5 * (u * u))
    tail = poly * t * bell
    cdf = jnp.where(u < 0, tail, 1.0 - tail)
    return u * cdf, cdf + u * ((2.0 * np.pi) ** -0.5 * bell)


def normalise(values):
    centred = values - jnp.mean(values, axis=-1, keepdims=True)
    inv_std = lax.rsqrt(jnp.mean(centred * centred, axis=-1, keepdims=True) + EPS)
    return centred * inv_std, inv_std


def norm_backward(grad_out, normed, inv_std, gain_vec):
    grad_normed = grad_out * gain_vec
    return inv_std * (
        grad_normed
        - jnp.mean(grad_normed, axis=-1, keepdims=True)
        - normed * jnp.mean(grad_normed * normed, axis=-1, keepdims=True)
    )


def row_chunks(rows, size, step):
    size = min(size, rows)

    @pl.loop(0, rows // size)
    def _(index):
        step(pl.ds(pl.multiple_of(index * size, size), size))


def split_rows(core, tile, rows, spots, keep, send):
    for block, spot in enumerate(spots):
        place = slice(spot * rows, (spot + 1) * rows)
        if rows % 8 == 0:
            own = pl.multiple_of((2 * block + core) * rows, 8)
            other = pl.multiple_of((2 * block + 1 - core) * rows, 8)
            keep[place, :] = tile[pl.ds(own, rows), :].astype(keep.dtype)
            send[place, :] = tile[pl.ds(other, rows), :].astype(send.dtype)
        else:
            even = tile[2 * block * rows : (2 * block + 1) * rows, :]
            odd = tile[(2 * block + 1) * rows : (2 * block + 2) * rows, :]
            keep[place, :] = jnp.where(core == 0, even, odd).astype(keep.dtype)
            send[place, :] = jnp.where(core == 0, odd, even).astype(send.dtype)


def attn_fwd_kernel(x_ref, w_ref, b_ref, dist_ref, mask_ref, *refs):
    qkv_ref, ctx_ref, p_ref, table = refs[-4:]
    length = x_ref.shape[0]
    width = 2 * length

    @pl.when(pl.program_id(1) == 0)
    def _():
        for head in range(2):
            row = jnp.broadcast_to(dist_ref[0, head : head + 1, :], (TILE, width))
            table[head] = pltpu.roll(row, 0, 1, stride=1, stride_axis=0)

    qkv = (contract(x_ref[...], w_ref[...], 1, 0) + b_ref[...]).astype(BF)
    qkv_ref[...] = qkv
    q = qkv[:, :PAIR] * jnp.asarray(HD**-0.5, BF)
    k = qkv[:, PAIR : 2 * PAIR]
    v = qkv[:, 2 * PAIR :]
    lane = lax.broadcasted_iota(jnp.int32, (length, PAIR), 1)
    raws = []
    for head in range(2):
        own = (lane < HD) == (head == 0)
        raws.append(contract(jnp.where(own, q, jnp.zeros_like(q)), k, 1, 1))
    outs = []
    for head in range(2):
        for start in range(0, length, TILE):
            half = start // (length // 2)
            logits = (
                raws[head][start : start + TILE]
                + table[head, :, length - start : width - start]
                + mask_ref[0, half : half + 1, :]
            )
            peak = jnp.max(logits, axis=1, keepdims=True)
            grown = jnp.exp(logits - peak)
            total = jnp.sum(grown, axis=1, keepdims=True)
            p_ref[0, head, start : start + TILE, :] = (grown * (1.0 / total)).astype(BF)
        outs.append(contract(p_ref[0, head], v, 1, 0))
    ctx_ref[...] = jnp.where(lane < HD, outs[0], outs[1]).astype(BF)


def attn_fwd(inputs, weight, bias, dist, mask, first, held):
    rows, width = inputs.shape
    micros = mask.shape[0]
    length = rows // micros
    pairs = weight.shape[1] // TRIO
    every = bias.shape[1] // TRIO
    return pl.pallas_call(
        attn_fwd_kernel,
        grid=(pairs, micros),
        in_specs=[
            pl.BlockSpec((length, width), lambda h, m: (m, 0)),
            pl.BlockSpec((width, TRIO), lambda h, m: (0, h)),
            pl.BlockSpec((1, TRIO), lambda h, m: (0, h + first)),
            pl.BlockSpec((1, 8, 2 * length), lambda h, m: (h + first, 0, 0)),
            pl.BlockSpec((1, 8, length), lambda h, m: (m, 0, 0)),
        ]
        + [pl.BlockSpec(memory_space=pl.ANY)] * len(held),
        out_specs=[
            pl.BlockSpec((length, TRIO), lambda h, m: (m, h + first)),
            pl.BlockSpec((length, PAIR), lambda h, m: (m, h + first)),
            pl.BlockSpec((1, 2, length, length), lambda h, m: (m, h + first, 0, 0)),
        ],
        out_shape=[
            jax.ShapeDtypeStruct((rows, every * TRIO), BF),
            jax.ShapeDtypeStruct((rows, every * PAIR), BF),
            jax.ShapeDtypeStruct((micros, 2 * every, length, length), BF),
        ],
        input_output_aliases={5 + index: index for index in range(len(held))},
        scratch_shapes=[pltpu.VMEM((2, TILE, 2 * length), F32)],
        compiler_params=pltpu.CompilerParams(vmem_limit_bytes=62 << 20),
        cost_estimate=cost(),
        name="attn_fwd",
    )(inputs, weight, bias, dist, mask, *held)


def attn_bwd_kernel(
    blocks, place_ref, qkv_ref, o_ref, dr_ref, p_ref, wo_ref, x_ref, *refs
):
    dqkv_ref, gd_ref, db_ref, keep_ref, send_ref, acc, dsb, dw, kept, sent = refs[-10:]
    length = qkv_ref.shape[0]
    width = 2 * length
    first = pl.program_id(1) == 0
    last = pl.program_id(1) == pl.num_programs(1) - 1

    @pl.when(first)
    def _():
        acc[...] = jnp.zeros_like(acc)
        dw[...] = jnp.zeros_like(dw)
        db_ref[...] = jnp.zeros_like(db_ref)

    q = qkv_ref[:, :PAIR]
    k = qkv_ref[:, PAIR : 2 * PAIR]
    v = qkv_ref[:, 2 * PAIR :]
    do = contract(dr_ref[...], wo_ref[...], 1, 1).astype(BF)
    lane = lax.broadcasted_iota(jnp.int32, (length, PAIR), 1)
    prod = do.astype(F32) * o_ref[...].astype(F32)
    dq, dk, dv, inners, dps = [], [], [], [], []
    for head in range(2):
        own = (lane < HD) == (head == 0)
        inners.append(jnp.sum(jnp.where(own, prod, 0.0), axis=1, keepdims=True))
        dps.append(contract(jnp.where(own, do, jnp.zeros_like(do)), v, 1, 1))
        dv.append(contract(p_ref[0, head], do, 0, 0))
    for head in range(2):
        inner, dp = inners[head], dps[head]
        for start in range(0, length, TILE):
            rows = slice(start, start + TILE)
            ds = p_ref[0, head, rows, :].astype(F32) * (dp[rows] - inner[rows])
            acc[head, :, length - start : width - start] += ds
            dsb[head, rows, :] = (ds * HD**-0.5).astype(BF)
        dq.append(contract(dsb[head], k, 1, 0))
        dk.append(contract(dsb[head], q, 0, 0))
    for index, (low, high) in enumerate((dq, dk, dv)):
        cols = slice(index * PAIR, (index + 1) * PAIR)
        grad = jnp.where(lane < HD, low, high).astype(BF)
        dqkv_ref[:, cols] = grad
        db_ref[0, 0:1, cols] += jnp.sum(grad.astype(F32), axis=0, keepdims=True)
    dw[...] += contract(x_ref[...], dqkv_ref[...], 0, 0)

    @pl.when(last)
    def _():
        split_rows(place_ref[3], dw, *blocks, kept, sent)
        keep_ref[...] = kept[...].astype(BF)
        send_ref[...] = sent[...].astype(BF)
        for head in range(2):
            total = acc[head, 0:8, :]
            for start in range(8, TILE, 8):
                total = total + pltpu.roll(acc[head, start : start + 8, :], width - start, 1)
            row = total[0:1, :]
            for step in range(1, 8):
                row = row + pltpu.roll(total[step : step + 1, :], width - step, 1)
            gd_ref[0, head : head + 1, :] = row


def attn_bwd(
    place, blocks, qkv, ctx, d_r, probs, w_output, inputs, first, pairs, held=(), start=0, every=None
):
    rows, width = inputs.shape
    micros, _, length, _ = probs.shape
    at = lambda shape, place: pl.BlockSpec(shape, lambda h, m, c: place(h, m))
    half = width // 2
    every = every or pairs
    return pl.pallas_call(
        partial(attn_bwd_kernel, blocks),
        grid_spec=pltpu.PrefetchScalarGridSpec(
            num_scalar_prefetch=1,
            grid=(pairs, micros),
            in_specs=[
                at((length, TRIO), lambda h, m: (m, h + first)),
                at((length, PAIR), lambda h, m: (m, h + first)),
                at((length, width), lambda h, m: (m, 0)),
                at((1, 2, length, length), lambda h, m: (m, h + first, 0, 0)),
                at((PAIR, width), lambda h, m: (h + first, 0)),
                at((length, width), lambda h, m: (m, 0)),
            ]
            + [pl.BlockSpec(memory_space=pl.ANY)] * len(held),
            out_specs=[
                at((length, TRIO), lambda h, m: (m, h + start)),
                at((1, 8, 2 * length), lambda h, m: (h + start, 0, 0)),
                at((1, 8, TRIO), lambda h, m: (h + start, 0, 0)),
                at((half, TRIO), lambda h, m: (0, h + start)),
                at((half, TRIO), lambda h, m: (0, h + start)),
            ],
            scratch_shapes=[
                pltpu.VMEM((2, TILE, 2 * length), F32),
                pltpu.VMEM((2, length, length), BF),
                pltpu.VMEM((width, TRIO), F32),
                pltpu.VMEM((half, TRIO), F32),
                pltpu.VMEM((half, TRIO), F32),
            ],
        ),
        out_shape=[
            jax.ShapeDtypeStruct((rows, every * TRIO), BF),
            jax.ShapeDtypeStruct((every, 8, 2 * length), F32),
            jax.ShapeDtypeStruct((every, 8, TRIO), F32),
            jax.ShapeDtypeStruct((half, every * TRIO), BF),
            jax.ShapeDtypeStruct((half, every * TRIO), BF),
        ],
        input_output_aliases={7 + index: index for index in range(len(held))},
        compiler_params=pltpu.CompilerParams(vmem_limit_bytes=62 << 20),
        cost_estimate=cost(),
        name="attn_bwd",
    )(place, qkv, ctx, d_r, probs, w_output, inputs, *held)


def vec(ref, name):
    return ref[ROW[name] : ROW[name] + 1, :]


def ffn_in_kernel(
    x_ref, ctx_ref, wo_ref, vec_ref, w_ref, b_ref, n1_ref, i1_ref, low_ref, act_ref, slope_ref
):
    rows = x_ref.shape[0]

    @pl.when(pl.program_id(0) == 0)
    def _():
        size = min(256, rows)
        for start in range(0, rows, size):
            at = slice(start, start + size)
            attn = contract(ctx_ref[at, :], wo_ref[...], 1, 0) + vec(vec_ref, "bias_attn")
            normed, inv_std = normalise(x_ref[at, :].astype(F32) + attn)
            n1_ref[at, :] = normed
            i1_ref[at, :] = inv_std
            first = normed * vec(vec_ref, "gain_attn") + vec(vec_ref, "shift_attn")
            low_ref[at, :] = first.astype(BF)

    def step(at):
        u = contract(low_ref[at, :], w_ref[...], 1, 0) + b_ref[...]
        act, slope = gelu_pair(u)
        act_ref[at, :] = act.astype(BF)
        slope_ref[at, :] = slope.astype(BF)

    row_chunks(rows, 256, step)


def ffn_in(inputs, context, w_output, vectors, w_inner, bias):
    rows, width = inputs.shape
    hidden = w_inner.shape[1]
    size = min(512, hidden)
    whole = pl.BlockSpec((rows, width), lambda n: (0, 0))
    column = pl.BlockSpec((rows, 1), lambda n: (0, 0))
    cols = pl.BlockSpec((rows, size), lambda n: (0, n))
    out = jax.ShapeDtypeStruct((rows, hidden), BF)
    return pl.pallas_call(
        ffn_in_kernel,
        grid=(hidden // size,),
        in_specs=[
            whole,
            whole,
            pl.BlockSpec((width, width), lambda n: (0, 0)),
            pl.BlockSpec((TABLE_ROWS, width), lambda n: (0, 0)),
            pl.BlockSpec((width, size), lambda n: (0, n)),
            pl.BlockSpec((1, size), lambda n: (0, n)),
        ],
        out_specs=[whole, column, whole, cols, cols],
        out_shape=[
            jax.ShapeDtypeStruct((rows, width), F32),
            jax.ShapeDtypeStruct((rows, 1), F32),
            jax.ShapeDtypeStruct((rows, width), BF),
            out,
            out,
        ],
        compiler_params=pltpu.CompilerParams(vmem_limit_bytes=62 << 20),
        cost_estimate=cost(),
        name="ffn_in",
    )(inputs, context, w_output, vectors, w_inner, bias)


def ffn_out_kernel(act_ref, w_ref, n1_ref, vec_ref, n2_ref, i2_ref, hid_ref, score_ref):
    first = n1_ref[...] * vec(vec_ref, "gain_attn") + vec(vec_ref, "shift_attn")
    outer = contract(act_ref[...], w_ref[...], 1, 0) + vec(vec_ref, "bias_outer")
    normed, inv_std = normalise(first + outer)
    n2_ref[...] = normed
    i2_ref[...] = inv_std
    low = (normed * vec(vec_ref, "gain_ffn") + vec(vec_ref, "shift_ffn")).astype(BF)
    hid_ref[...] = low
    row = low[0:8, :].astype(F32)[0:1, :] * vec(vec_ref, "w_score")
    score_ref[0] = jnp.broadcast_to(jnp.sum(row, axis=1, keepdims=True), score_ref.shape[1:])


def ffn_out(act, w_outer, normed, vectors, count):
    rows, hidden = act.shape
    width = w_outer.shape[1]
    size = rows // count
    block = pl.BlockSpec((size, width), lambda r: (r, 0))
    return pl.pallas_call(
        ffn_out_kernel,
        grid=(count,),
        in_specs=[
            pl.BlockSpec((size, hidden), lambda r: (r, 0)),
            pl.BlockSpec((hidden, width), lambda r: (0, 0)),
            block,
            pl.BlockSpec((TABLE_ROWS, width), lambda r: (0, 0)),
        ],
        out_specs=[
            block,
            pl.BlockSpec((size, 1), lambda r: (r, 0)),
            block,
            pl.BlockSpec((1, 8, 128), lambda r: (r, 0, 0)),
        ],
        out_shape=[
            jax.ShapeDtypeStruct((rows, width), F32),
            jax.ShapeDtypeStruct((rows, 1), F32),
            jax.ShapeDtypeStruct((rows, width), BF),
            jax.ShapeDtypeStruct((count, 8, 128), F32),
        ],
        compiler_params=pltpu.CompilerParams(vmem_limit_bytes=62 << 20),
        cost_estimate=cost(),
        name="ffn_out",
    )(act, w_outer, normed, vectors)


def list_loss(scores, lens, relevance):
    present = lens > 0
    masked = jnp.where(present, scores, NEG)
    peak = jnp.max(masked, axis=1, keepdims=True)
    log_total = peak + jnp.log(jnp.sum(jnp.exp(masked - peak), axis=1, keepdims=True))
    log_prob = masked - log_total
    rel = jnp.where(present, relevance, NEG)
    rel_exp = jnp.exp(rel - jnp.max(rel, axis=1, keepdims=True))
    target = rel_exp / jnp.sum(rel_exp, axis=1, keepdims=True)
    loss = -jnp.sum(jnp.where(present, target * log_prob, 0.0), axis=1, keepdims=True)
    return loss, jnp.where(present, jnp.exp(log_prob) - target, 0.0)


def outer_bwd_kernel(
    blocks, place_ref, score_ref, len_ref, rel_ref, cot_ref, n2_ref, i2_ref, hid_ref, vec_ref,
    act_ref, dr_ref, low, sum_ref, loss_ref, keep_ref, send_ref, tile, kept, sent,
):
    rows, width = cot_ref.shape

    @pl.when(pl.program_id(0) == 0)
    def _():
        loss, grad = list_loss(score_ref[...], len_ref[...], rel_ref[...])
        loss_ref[...] = jnp.broadcast_to(loss, loss_ref.shape)
        lane = lax.broadcasted_iota(jnp.int32, grad.shape, 1)
        micros = grad.shape[0]
        sum_ref[...] = jnp.zeros_like(sum_ref)
        firsts = {}
        for half in range(2):
            own = jnp.where(lane == 2 * place_ref[4] + half, grad, 0.0)
            own = jnp.sum(own, axis=1, keepdims=True)
            for micro in range(micros):
                firsts[(2 * micro + half) * (rows // (2 * micros))] = own[micro : micro + 1, :]
        score_row = vec(vec_ref, "w_score")
        gain = vec(vec_ref, "gain_ffn")

        def step(at):
            grad_out = cot_ref[at, :].astype(F32)
            place = lax.broadcasted_iota(jnp.int32, (grad_out.shape[0], 1), 0) + at.start
            shift = jnp.zeros_like(place, F32)
            for first, value in firsts.items():
                shift = jnp.where(place == first, value, shift)
            grad_out = grad_out + shift * score_row
            normed = n2_ref[at, :]
            grad_in = norm_backward(grad_out, normed, i2_ref[at, :], gain)
            dr_ref[at, :] = grad_in
            grad_low = grad_in.astype(BF)
            low[at, :] = grad_low
            sum_ref[0:1, :] += jnp.sum(grad_out * normed, axis=0, keepdims=True)
            sum_ref[1:2, :] += jnp.sum(grad_out, axis=0, keepdims=True)
            sum_ref[2:3, :] += jnp.sum(grad_low.astype(F32), axis=0, keepdims=True)

        row_chunks(rows, 128, step)
        total = jnp.zeros((1, width), F32)
        for first, value in firsts.items():
            total = total + value * hid_ref[first : first + 8, :].astype(F32)[0:1, :]
        sum_ref[3:4, :] = total

    tile[...] = contract(act_ref[...], low[...], 0, 0)
    split_rows(place_ref[3], tile, *blocks, kept, sent)
    keep_ref[...] = kept[...].astype(BF).reshape(keep_ref.shape)
    send_ref[...] = sent[...].astype(BF).reshape(send_ref.shape)


def outer_bwd(
    place, blocks, scores, lens, relevance, cot, normed, inv_std, hid, vectors, act
):
    rows, width = cot.shape
    hidden = act.shape[1]
    size = width
    at = lambda shape, index: pl.BlockSpec(shape, lambda n, c: index(n))
    whole = at((rows, width), lambda n: (0, 0))
    tiny = at(scores.shape, lambda n: (0, 0))
    rows_of, spots = blocks
    tiles = hidden // size
    half = at((len(spots), 1, rows_of, width), lambda n: (0, n, 0, 0))
    return pl.pallas_call(
        partial(outer_bwd_kernel, blocks),
        grid_spec=pltpu.PrefetchScalarGridSpec(
            num_scalar_prefetch=1,
            grid=(hidden // size,),
            in_specs=[
                tiny, tiny, tiny, whole, whole, at((rows, 1), lambda n: (0, 0)), whole,
                at((TABLE_ROWS, width), lambda n: (0, 0)), at((rows, size), lambda n: (0, n)),
            ],
            out_specs=[
                whole, whole, at((8, width), lambda n: (0, 0)),
                at((scores.shape[0], 128), lambda n: (0, 0)), half, half,
            ],
            scratch_shapes=[
                pltpu.VMEM((size, width), F32),
                pltpu.VMEM((size // 2, width), F32),
                pltpu.VMEM((size // 2, width), F32),
            ],
        ),
        out_shape=[
            jax.ShapeDtypeStruct((rows, width), F32),
            jax.ShapeDtypeStruct((rows, width), BF),
            jax.ShapeDtypeStruct((8, width), F32),
            jax.ShapeDtypeStruct((scores.shape[0], 128), F32),
            jax.ShapeDtypeStruct((len(spots), tiles, rows_of, width), BF),
            jax.ShapeDtypeStruct((len(spots), tiles, rows_of, width), BF),
        ],
        compiler_params=pltpu.CompilerParams(vmem_limit_bytes=62 << 20),
        cost_estimate=cost(),
        name="outer_bwd",
    )(place, scores, lens, relevance, cot, normed, inv_std, hid, vectors, act)


def act_bwd_kernel(dr_ref, slope_ref, w2_ref, din_ref, db_ref):
    grad = dr_ref[...]
    wide = w2_ref.shape[0]
    size = min(256, wide)
    for start in range(0, wide, size):
        cols = slice(start, start + size)
        d_act = contract(grad, w2_ref[cols, :], 1, 1)
        d_in = (d_act * slope_ref[:, cols].astype(F32)).astype(BF)
        din_ref[:, cols] = d_in
        db_ref[:, cols] = jnp.sum(d_in.astype(F32), axis=0, keepdims=True)


def act_bwd(grad, slope, w_outer):
    rows, hidden = slope.shape
    width = grad.shape[1]
    size = min(512, hidden)
    cols = pl.BlockSpec((rows, size), lambda n: (0, n))
    return pl.pallas_call(
        act_bwd_kernel,
        grid=(hidden // size,),
        in_specs=[
            pl.BlockSpec((rows, width), lambda n: (0, 0)),
            cols,
            pl.BlockSpec((size, width), lambda n: (n, 0)),
        ],
        out_specs=[cols, pl.BlockSpec((1, size), lambda n: (0, n))],
        out_shape=[
            jax.ShapeDtypeStruct((rows, hidden), BF),
            jax.ShapeDtypeStruct((1, hidden), F32),
        ],
        compiler_params=pltpu.CompilerParams(vmem_limit_bytes=62 << 20),
        cost_estimate=cost(),
        name="act_bwd",
    )(grad, slope, w_outer)


def inner_bwd_kernel(
    blocks, place_ref, din_ref, w1_ref, low_ref, dr_ref, n1_ref, i1_ref, vec_ref, ctx_ref,
    one_ref, grad_ref, sum_ref, keep_ref, send_ref, acc, tile, kept, sent,
):
    step_id = pl.program_id(0)
    last = pl.num_programs(0) - 1
    rows = low_ref.shape[0]

    @pl.when(step_id < last)
    def _():
        d_in = din_ref[...]
        tile[...] = contract(low_ref[...], d_in, 0, 0)
        part = contract(d_in, w1_ref[...], 1, 1)

        @pl.when(step_id == 0)
        def _():
            acc[...] = dr_ref[...] + part

        @pl.when(step_id > 0)
        def _():
            acc[...] += part

    @pl.when(step_id == last)
    def _():
        sum_ref[...] = jnp.zeros_like(sum_ref)
        gain = vec(vec_ref, "gain_attn")

        def step(at):
            grad_out = acc[at, :]
            normed = n1_ref[at, :]
            grad_in = norm_backward(grad_out, normed, i1_ref[at, :], gain)
            one_ref[at, :] = grad_in
            grad_low = grad_in.astype(BF)
            grad_ref[at, :] = grad_low
            sum_ref[0:1, :] += jnp.sum(grad_out * normed, axis=0, keepdims=True)
            sum_ref[1:2, :] += jnp.sum(grad_out, axis=0, keepdims=True)
            sum_ref[2:3, :] += jnp.sum(grad_low.astype(F32), axis=0, keepdims=True)

        row_chunks(rows, 128, step)
        tile[...] = contract(ctx_ref[...], grad_ref[...], 0, 0)

    split_rows(place_ref[3], tile, *blocks, kept, sent)
    keep_ref[...] = kept[...].astype(BF)
    send_ref[...] = sent[...].astype(BF)


def inner_bwd(place, blocks, d_in, w_inner, low, d_r, normed, inv_std, vectors, context):
    rows, width = low.shape
    hidden = d_in.shape[1]
    size = width
    tiles = hidden // size
    at = lambda shape, index: pl.BlockSpec(shape, lambda n, c: index(n))
    whole = at((rows, width), lambda n: (0, 0))
    near = lambda n: (0, jnp.minimum(n, tiles - 1))
    half = at((width // 2, size), lambda n: (0, n))
    return pl.pallas_call(
        partial(inner_bwd_kernel, blocks),
        grid_spec=pltpu.PrefetchScalarGridSpec(
            num_scalar_prefetch=1,
            grid=(tiles + 1,),
            in_specs=[
                at((rows, size), near), at((width, size), near), whole, whole, whole,
                at((rows, 1), lambda n: (0, 0)), at((TABLE_ROWS, width), lambda n: (0, 0)), whole,
            ],
            out_specs=[whole, whole, at((8, width), lambda n: (0, 0)), half, half],
            scratch_shapes=[
                pltpu.VMEM((rows, width), F32),
                pltpu.VMEM((width, size), F32),
                pltpu.VMEM((width // 2, size), F32),
                pltpu.VMEM((width // 2, size), F32),
            ],
        ),
        out_shape=[
            jax.ShapeDtypeStruct((rows, width), F32),
            jax.ShapeDtypeStruct((rows, width), BF),
            jax.ShapeDtypeStruct((8, width), F32),
            jax.ShapeDtypeStruct((width // 2, hidden + width), BF),
            jax.ShapeDtypeStruct((width // 2, hidden + width), BF),
        ],
        compiler_params=pltpu.CompilerParams(vmem_limit_bytes=62 << 20),
        cost_estimate=cost(),
        name="inner_bwd",
    )(place, d_in, w_inner, low, d_r, normed, inv_std, vectors, context)


def shifted(axis_size, group, stride, step):
    pairs = []
    for source in range(axis_size):
        place = source // stride % group
        pairs.append((source, source + ((place + step) % group - place) * stride))
    return pairs


class Grid:
    def __init__(self, query_size, cand_size):
        query, cand = lax.axis_index("query"), lax.axis_index("cand")
        self.sizes = {"outer": query_size // 2, "inner": 2, "far": cand_size // 2, "core": 2}
        self.lengths = {"query": query_size, "cand": cand_size}
        self.axes = {
            "outer": ("query", 2),
            "inner": ("query", 1),
            "far": ("cand", 2),
            "core": ("cand", 1),
        }
        self.at = {
            "outer": query // 2,
            "inner": query % 2,
            "far": cand // 2,
            "core": cand % 2,
        }

    def move(self, value, dim, step):
        axis, stride = self.axes[dim]
        return lax.ppermute(
            value, axis, shifted(self.lengths[axis], self.sizes[dim], stride, step)
        )


def pack_kernel(pairs, place_ref, wq, wk, wv, wo, table, first, middle):
    far, core = place_ref[2], place_ref[3]
    half = wq.shape[0] // 2
    rows = pl.ds(pl.multiple_of(core * half, 16), half)
    for pair in range(pairs):
        for index, weight in enumerate((wq, wk, wv)):
            to = (pair * 3 + index) * PAIR
            first[:half, to : to + PAIR] = weight[rows, pair * PAIR : (pair + 1) * PAIR]
    first[half:, :] = table[...]
    count = wq.shape[1] // PAIR // pairs - 1
    for run in range(count):
        cols = pl.ds(pl.multiple_of(((run + 1) * pairs + far) * PAIR, PAIR), PAIR)
        for index, weight in enumerate((wq, wk, wv)):
            middle[run * half : (run + 1) * half, index * PAIR : (index + 1) * PAIR] = weight[rows, cols]
    wide = wo.shape[1] // 2
    cols = pl.ds(pl.multiple_of(far * wide, PAIR), wide)
    middle[count * half :, :] = wo[rows, cols]


def pack(place, pairs, wq, wk, wv, wo, table):
    shard, width = wq.shape
    half = shard // 2
    count = width // PAIR // pairs
    shapes = [
        (half + TABLE_ROWS, pairs * TRIO),
        (count * half, width // 2),
    ]
    return pl.pallas_call(
        partial(pack_kernel, pairs),
        grid_spec=pltpu.PrefetchScalarGridSpec(
            num_scalar_prefetch=1,
            grid=(1,),
            in_specs=[
                pl.BlockSpec(value.shape, lambda i, c: (0, 0)) for value in (wq, wk, wv, wo, table)
            ],
            out_specs=[pl.BlockSpec(shape, lambda i, c: (0, 0)) for shape in shapes],
        ),
        out_shape=[jax.ShapeDtypeStruct(shape, BF) for shape in shapes],
        compiler_params=pltpu.CompilerParams(vmem_limit_bytes=60 << 20),
        cost_estimate=cost(),
        name="pack",
    )(place, wq, wk, wv, wo, table)


def join_kernel(runs, count, *refs):
    sources, targets = refs[:count], refs[count:]
    at = 0
    for source in sources:
        size = source.shape[0]
        for target, (first, rows) in zip(targets, runs):
            target[at : at + size] = source[:, first : first + rows, :]
        at += size


def join(pieces, runs):
    total = sum(piece.shape[0] for piece in pieces)
    wide = pieces[0].shape[2]
    whole = lambda shape: pl.BlockSpec(shape, lambda i: (0, 0, 0))
    shapes = [(total, rows, wide) for _, rows in runs]
    return pl.pallas_call(
        partial(join_kernel, runs, len(pieces)),
        grid=(1,),
        in_specs=[whole(piece.shape) for piece in pieces],
        out_specs=[whole(shape) for shape in shapes],
        out_shape=[jax.ShapeDtypeStruct(shape, BF) for shape in shapes],
        compiler_params=pltpu.CompilerParams(vmem_limit_bytes=62 << 20),
        cost_estimate=cost(),
        name="join",
    )(*pieces)


class Gather:
    def __init__(self, grid, blocks, places=None):
        self.grid = grid
        self.pieces = [blocks]
        self.places = [places or [{"outer": 0, "inner": 0, "far": 0, "core": 0}]]
        self.received = []

    def joined(self, *runs):
        places = sum(self.places, [])
        runs = runs or ((0, self.pieces[0].shape[1]),)
        return [Gather(self.grid, piece, places) for piece in join(self.pieces, runs)]

    def start(self, dim):
        size = self.grid.sizes[dim]
        self.coming = []
        for piece, places in zip(self.pieces, self.places):
            for step in range(1, size):
                self.received.append(self.grid.move(piece, dim, step))
                self.coming.append(
                    [{**place, dim: (place[dim] + step) % size} for place in places]
                )

    def fold(self):
        self.pieces = self.pieces + self.received
        self.places = self.places + self.coming
        self.received = []


def place_kernel(splits, places, outer, spot_ref, *refs):
    count = 1 + max(run[0] for split in splits for run in split)
    sources, targets, sems = refs[: -1 - count], refs[-1 - count : -1], refs[-1]
    copies = []
    at = 0
    for source, split in zip(sources, splits):
        wide = source.shape[-1]
        for index in range(source.shape[0]):
            place = places[at]
            zed = lax.rem(spot_ref[0] + (outer - place["outer"]), outer)
            other = {
                dim: lax.rem(spot_ref[i] + place[dim], 2)
                for i, dim in enumerate(("inner", "far", "core"), 1)
            }
            block = (zed * 2 + other["inner"]) * 2 + other["core"]
            first = 0
            for target, rows, stride, offset in split:
                cols = slice(None)
                if stride:
                    col = other["far"] * (stride * wide) + offset * wide
                    cols = pl.ds(pl.multiple_of(col, 128), wide)
                copies.append(
                    pltpu.make_async_copy(
                        source.at[index, pl.ds(first, rows), :],
                        targets[target].at[pl.ds(pl.multiple_of(block * rows, 16), rows), cols],
                        sems.at[len(copies)],
                    )
                )
                first += rows
            at += 1
    for copy in copies:
        copy.start()
    for copy in copies:
        copy.wait()


def place_blocks(spot, shapes, *gathers):
    places, pieces, splits, copies = [], [], [], 0
    for gather, split in gathers:
        for piece, found in zip(gather.pieces, gather.places):
            pieces.append(piece)
            splits.append(split)
            places += found
            copies += len(found) * len(split)
    return pl.pallas_call(
        partial(place_kernel, splits, places, gather.grid.sizes["outer"]),
        grid_spec=pltpu.PrefetchScalarGridSpec(
            num_scalar_prefetch=1,
            grid=(1,),
            in_specs=[pl.BlockSpec(memory_space=pl.ANY)] * len(pieces),
            out_specs=[pl.BlockSpec(memory_space=pltpu.VMEM)] * len(shapes),
            scratch_shapes=[pltpu.SemaphoreType.DMA((copies,))],
        ),
        out_shape=[jax.ShapeDtypeStruct(shape, BF) for shape in shapes],
        compiler_params=pltpu.CompilerParams(vmem_limit_bytes=24 << 20),
        cost_estimate=cost(),
        name="place_blocks",
    )(spot, *pieces)


class Scatter:
    def __init__(self, grid, keep, send, order):
        self.grid = grid
        self.dims = list(order)
        self.order = list(order)
        self.sizes = [grid.sizes[dim] for dim in self.dims]
        self.rider, self.others = None, ()
        self.parts = [self.blocks(keep)]
        self.shape = self.blocks(send).shape
        self.received = [grid.move(send, "core", 1)]

    def blocks(self, value):
        return value.reshape(*self.sizes, -1, value.shape[-1])

    @staticmethod
    def spots(grid, order, tiles=1):
        sizes = {dim: grid.sizes[dim] for dim in order}
        if tiles > 1:
            sizes["outer"] //= tiles
        spots = []
        for block in range(int(np.prod(list(sizes.values())))):
            at = {
                "outer": block // (2 * sizes["far"]),
                "inner": block // sizes["far"] % 2,
                "far": block % sizes["far"],
            }
            spot = 0
            for dim in order:
                spot = spot * sizes[dim] + at[dim]
            spots.append(spot)
        return tuple(spots)

    def step(self, dim):
        axis = self.dims.index(dim)
        size, here = self.grid.sizes[dim], self.grid.at[dim]
        sent = []
        for step in range(1, size):
            total = 0.0
            for part in self.parts:
                piece = lax.dynamic_index_in_dim(part, (here + step) % size, axis, keepdims=False)
                total += piece.astype(F32)
            sent.append(total.astype(BF))
        self.parts = [
            lax.dynamic_index_in_dim(part, here, axis, keepdims=False) for part in self.parts
        ]
        self.dims.remove(dim)
        return sent

    def start(self, *others):
        dim = self.order.pop(0)
        sent = self.step(dim)
        self.others = others
        self.shape = sent[0].shape
        for other in others:
            other.order.remove(dim)
            more = other.step(dim)
            other.shape = more[0].shape
            sent = [jnp.concatenate(pair, axis=-1) for pair in zip(sent, more)]
        if self.rider is not None:
            wide = sent[0].shape[-1]
            rider = jnp.pad(self.rider, ((0, 0), (0, wide - self.rider.shape[1]))).astype(BF)
            sent = [jnp.concatenate([value.reshape(-1, wide), rider]) for value in sent]
        self.received = [self.grid.move(value, dim, step) for step, value in enumerate(sent, 1)]

    def fold(self):
        for value in self.received:
            if self.rider is not None:
                count = value.shape[0] - self.rider.shape[0]
                self.rider = self.rider + value[count:, : self.rider.shape[1]].astype(F32)
                value = value[:count]
            value = value.reshape(*self.shape[:-1], value.shape[-1])
            at = 0
            for scatter in (self, *self.others):
                wide = scatter.shape[-1]
                scatter.parts.append(value[..., at : at + wide])
                at += wide
        self.received, self.others = [], ()

    def result(self):
        while self.order:
            self.start()
            self.fold()
        return sum(part.astype(F32) for part in self.parts)


def after(values, *steps):
    moved = [piece for step in steps for piece in step.received]
    count = len(values)
    held = lax.optimization_barrier((*values, *moved))
    values, moved = held[:count], list(held[count:])
    for step in steps:
        count = len(step.received)
        step.received, moved = moved[:count], moved[count:]
        step.fold()
    return values


def key_masks(lens, length):
    middle = length // 2
    places = jnp.arange(length, dtype=jnp.int32)
    first, second = lens[:, :1], lens[:, 1:]
    single = places < first
    low = jnp.where(second > 0, single & (places < middle), single)
    high = jnp.where(second > 0, (places >= middle) & (places - middle < second), single)
    mask = jnp.where(jnp.stack([low, high], axis=1), 0.0, NEG)
    return jnp.pad(mask, ((0, 0), (0, 6), (0, 0)))


def body(
    sizes,
    tokens,
    cotangent,
    lengths,
    relevance,
    rel_table,
    w_query,
    w_key,
    w_value,
    w_output,
    w_inner,
    w_outer,
    bias_query,
    bias_value,
    bias_attn,
    bias_inner,
    bias_outer,
    gain_attn,
    shift_attn,
    gain_ffn,
    shift_ffn,
    rel_bias,
    w_score,
):
    query_size, cand_size = sizes
    devices = query_size * cand_size
    grid = Grid(query_size, cand_size)
    both = ("query", "cand")
    own_slot = lax.axis_index("cand")
    micros, length, width = tokens.shape[0], tokens.shape[3], tokens.shape[4]
    heads = rel_bias.shape[1]
    buckets = rel_bias.shape[0] * query_size
    pairs = heads // 2
    group_pairs = pairs // 3
    shard = w_query.shape[0]
    hidden = w_inner.shape[1]
    inner_shard = bias_inner.shape[0]
    spot = jnp.stack([*(grid.at[dim] for dim in ("outer", "inner", "far", "core")), own_slot])
    spot = spot.astype(jnp.int32)

    def own_part(value):
        rows = value.shape[0] // cand_size
        return lax.dynamic_slice_in_dim(value, own_slot * rows, rows, 0)

    def padded(row):
        row = row.reshape(1, -1)
        return jnp.pad(row, ((0, 0), (0, width - row.shape[1])))

    own_lens = lax.dynamic_index_in_dim(lengths[:, 0], own_slot, 1, keepdims=False)
    mask = key_masks(own_lens, length)
    lens_row = lengths.reshape(micros, 2 * cand_size)
    rel_row = relevance.reshape(micros, 2 * cand_size)
    vectors = (
        bias_query, bias_value, bias_attn, bias_outer, gain_attn, shift_attn, gain_ffn, shift_ffn,
        w_score,
    )
    table = jnp.stack(vectors)
    table = jnp.concatenate(
        [
            jnp.pad(table, ((0, 0), (0, width - shard))),
            padded(bias_inner),
            padded(rel_bias),
            jnp.zeros((TABLE_ROWS - len(VECTORS) - 2, width), BF),
        ]
    )
    groups = (group_pairs, pairs - group_pairs)
    w_inner = lax.all_gather(own_part(w_inner), both, axis=0, tiled=True)
    w_outer = lax.all_gather(own_part(w_outer), both, axis=0, tiled=True)
    stepped = shard % 32 == 0 and width // grid.sizes["far"] == TRIO == PAIR * (pairs // 2)
    if stepped:
        half = shard // 2
        blocks = pack(spot, group_pairs, w_query, w_key, w_value, w_output, table)
        head = Gather(grid, blocks[0][None])
        head.start("outer")
        lens_row, rel_row, mask = after((lens_row, rel_row, mask), head)
        (head,) = head.joined()
        block, head.pieces[0] = lax.optimization_barrier((blocks[1], head.pieces[0]))
        rest = Gather(grid, block[None])
        head.start("inner")
        rest.start("outer")
        after((), head, rest)
        head.start("core")
        near_part, far_part = rest.joined((0, half), (half, block.shape[0] - half))
        near_part.start("inner")
        far_part.start("far")
        after((), head)
        shapes = ((width, group_pairs * TRIO), (2 * query_size * TABLE_ROWS, width))
        first_weight, table = place_blocks(
            spot, shapes, (head, ((0, half, 0, 0), (1, TABLE_ROWS, 0, 0)))
        )
        table = table.reshape(query_size, 2, TABLE_ROWS, width)[:, 0]
    else:
        packed = jnp.stack(
            [value.reshape(shard, pairs, PAIR) for value in (w_query, w_key, w_value)], axis=2
        ).reshape(shard, pairs * TRIO)
        gather = partial(lax.all_gather, axis_name="query", axis=0, tiled=True)
        first_weight = gather(packed[:, : group_pairs * TRIO])
        second_weight = gather(packed[:, group_pairs * TRIO :])
        w_output = gather(w_output)
        table = gather(table).reshape(query_size, TABLE_ROWS, width)

    count = len(VECTORS)
    bias_inner = table[:, count, :inner_shard].reshape(1, hidden).astype(F32)
    rel_bias = table[:, count + 1, : rel_bias.size].reshape(buckets, heads)
    table = table[:, :count, :shard].transpose(1, 0, 2).reshape(count, width).astype(F32)
    bias_qkv = jnp.stack(
        [
            table[0].reshape(pairs, PAIR),
            jnp.zeros((pairs, PAIR), F32),
            table[1].reshape(pairs, PAIR),
        ],
        axis=1,
    ).reshape(1, pairs * TRIO)
    table = jnp.pad(table, ((0, TABLE_ROWS - count), (0, 0)))

    one_hot = (rel_table[:, None] == jnp.arange(buckets, dtype=jnp.int32)[None, :]).astype(BF)
    one_hot = jnp.pad(one_hot, ((1, 0), (0, 0)))
    dist = contract(rel_bias, one_hot, 0, 1).reshape(pairs, 2, 2 * length)
    dist = jnp.pad(dist, ((0, 0), (0, 6), (0, 0)))

    inputs = tokens.reshape(micros * length, width)
    if stepped:
        first_weight, bias_qkv, dist, table, bias_inner = after(
            (first_weight, bias_qkv, dist, table, bias_inner), near_part, far_part
        )
        (near_part,), (far_part,) = near_part.joined(), far_part.joined()
        near_part.start("far")
        far_part.start("inner")
    held = attn_fwd(inputs, first_weight, bias_qkv, dist, mask, 0, ())
    if stepped:
        held = after(held, near_part, far_part)
        near_part.start("core")
        far_part.start("core")
        held = after(held, near_part, far_part)
        second_weight, w_output = place_blocks(
            spot,
            ((width, groups[1] * TRIO), (width, width)),
            (near_part, ((0, half, 1, 0),)),
            (far_part, ((0, half, 1, 2), (1, half, 1, 0))),
        )
    qkv, context, probs = attn_fwd(
        inputs, second_weight, bias_qkv, dist, mask, group_pairs, held
    )
    normed_one, inv_one, low, act, slope = ffn_in(
        inputs, context, w_output, table, w_inner, bias_inner
    )
    act, w_outer = lax.optimization_barrier((act, w_outer))
    normed_two, inv_two, hidden_out, scores = ffn_out(act, w_outer, normed_one, table, 2 * micros)

    all_scores = lax.all_gather(
        scores[:, 0, 0].reshape(micros, 1, 2), "cand", axis=1, tiled=True
    ).reshape(micros, 2 * cand_size)
    block_rows = width // devices
    by_far, by_inner = ("far", "inner", "outer"), ("inner", "far", "outer")
    tiles = hidden // width
    grad_two, grad_outer, sums_two, loss, keep, send = outer_bwd(
        spot,
        (hidden // devices, Scatter.spots(grid, by_far, tiles)),
        all_scores,
        lens_row,
        rel_row,
        cotangent.reshape(micros * length, width),
        normed_two,
        inv_two,
        hidden_out,
        table,
        act,
    )
    far_blocks = (block_rows, Scatter.spots(grid, by_far))
    inner_blocks = (block_rows, Scatter.spots(grid, by_inner))
    sum_outer = Scatter(grid, keep, send, by_far)
    grad_in, grad_bias_inner = after(act_bwd(grad_outer, slope, w_outer), sum_outer)
    sum_outer.start()
    grad_one, grad_attn, sums_one, keep, send = after(
        inner_bwd(
            spot, inner_blocks, grad_in, w_inner, low, grad_two, normed_one, inv_one, table, context
        ),
        sum_outer,
    )
    sum_inner = Scatter(grid, keep, send, by_inner)
    sum_outer.start()
    *early, grad_attn = after(
        (
            *attn_bwd(
                spot, far_blocks, qkv, context, grad_attn, probs, w_output, inputs, 0, group_pairs
            ),
            grad_attn,
        ),
        sum_outer,
        sum_inner,
    )
    grad_qkv, dist_grad, bias_grad, keep, send = early
    sum_early = Scatter(grid, keep, send, by_far)
    sum_inner.start()
    sum_outer.start()
    (grad_attn,) = after((grad_attn,), sum_early)
    sum_early.start()
    late = attn_bwd(
        spot, inner_blocks, qkv, context, grad_attn, probs, w_output, inputs, group_pairs,
        pairs - group_pairs,
    )
    others = (grad_qkv, dist_grad, bias_grad, grad_bias_inner, sums_one, sums_two, loss)
    late = after((*late, *others), sum_early, sum_outer, sum_inner)
    late_qkv, late_dist, late_bias, keep, send = late[:5]
    grad_qkv, dist_grad, bias_grad, grad_bias_inner, sums_one, sums_two, loss = late[5:]
    sum_late = Scatter(grid, keep, send, by_inner)
    sum_inner.start()
    sum_early.start()

    dist_grad = jnp.concatenate([dist_grad, late_dist])[:, :2].reshape(heads, 2 * length)
    grad_rel = lax.dot_general(
        dist_grad,
        one_hot.astype(F32),
        (((1,), (0,)), ((), ())),
        precision=lax.Precision.HIGHEST,
    )
    bias_grad = jnp.concatenate([bias_grad, late_bias])[:, 0].reshape(pairs, 3, PAIR)
    small = [
        sums_one[:3],
        sums_two[:4],
        bias_grad.transpose(1, 0, 2).reshape(3, width),
        grad_bias_inner.reshape(-1, width),
        jnp.pad(grad_rel, ((0, 0), (0, width - buckets))),
    ]
    rows = sum(value.shape[0] for value in small)
    fold = keep.shape[1] // width
    small.append(jnp.zeros((-rows % (8 * fold), width), F32))
    small = jnp.concatenate(small)
    rows = small.shape[0] // fold
    rider = jnp.concatenate([small[i * rows : (i + 1) * rows] for i in range(fold)], axis=1)
    grad_qkv, late_qkv, rider = after((grad_qkv, late_qkv, rider), sum_late)
    sum_late.start()
    rider = rider + grid.move(rider.astype(BF), "core", 1).astype(F32)
    other = grid.move(rider.astype(BF), "inner", 1)
    grad_inputs = grad_one + contract(grad_qkv, first_weight, 1, 1)
    grad_inputs = grad_inputs + contract(late_qkv, second_weight, 1, 1)
    grad_inputs, other = after((grad_inputs, other), sum_early, sum_inner)
    sum_inner.start()
    after((), sum_late)
    sum_late.rider = rider + other.astype(F32)
    sum_late.start()
    after((), sum_late)
    sum_late.start(sum_early)
    after((), sum_inner)
    after((), sum_late)
    own_late = sum_late.result()
    own_early = sum_early.result()
    own_outer = sum_outer.result()
    own_inner = sum_inner.result()
    own = jnp.concatenate([own_early, own_late], axis=1).reshape(block_rows, pairs, 3, PAIR)
    own_query, own_key, own_value = [own[:, :, i].reshape(-1, width) for i in range(3)]

    small = jnp.concatenate(
        [sum_late.rider[:, i * width : (i + 1) * width] for i in range(fold)], axis=0
    )
    index = lax.axis_index("query") * cand_size + own_slot
    small_own = lax.dynamic_slice_in_dim(small, index * block_rows, block_rows, 1)
    at = 10 + hidden // width
    flat = small[10:at].reshape(-1)
    own_bias_inner = lax.dynamic_slice_in_dim(flat, index * (hidden // devices), hidden // devices)
    rel_rows = buckets // devices
    own_rel = lax.dynamic_slice_in_dim(small[at : at + heads], index * rel_rows, rel_rows, 1)
    shape = (micros, 1, 1, length, width)
    return (
        hidden_out.reshape(shape),
        loss[:, :1],
        grad_inputs.reshape(shape),
        own_query,
        own_key,
        own_value,
        own_inner[:, hidden:],
        own_inner[:, :hidden],
        own_outer,
        small_own[7],
        small_own[9],
        small_own[2],
        own_bias_inner,
        small_own[5],
        small_own[0],
        small_own[1],
        small_own[3],
        small_own[4],
        own_rel.T,
        small_own[6],
    )


def solution(mesh):
    both = ("query", "cand")
    slots = P(None, "query", "cand", None, None)
    lists = P(None, "query", None, None)
    rows = P("query", None)
    vec_spec = P("query")
    return jax.shard_map(
        partial(body, (mesh.shape["query"], mesh.shape["cand"])),
        mesh=mesh,
        in_specs=(slots, slots, lists, lists, P()) + (rows,) * 6 + (vec_spec,) * 9 + (rows, vec_spec),
        out_specs=(slots, P(None, "query"), slots)
        + (P(both, None),) * 6
        + (P(both),) * 9
        + (P(both, None), P(both)),
        check_vma=False,
    )
```

profile of v0, /device:TPU:9, one launch (start us, length us, event | category | flops | bytes accessed | tf_op | source)
XLA Modules:
  0.0 366.5 jit_solution(17297724460938385256)
XLA Ops:
  9.0 1.6 constant_dynamic-slice_fusion.1
  12.9 1.5 stack.71
  15.1 2.5 pack.1
  19.9 1.5 collective-permute-start.2
  26.2 1.8 collective-permute-done.1.refs_2_
  28.1 3.5 collective-permute-done.2.refs_3_
  32.3 1.8 join.4.refs_0_
  35.3 1.7 collective-permute-start.5
  37.5 3.3 collective-permute-start.7
  40.8 2.3 collective-permute-done.5.refs_2_
  43.1 8.8 %collective-permute-done.6.refs_3_ = bf16[1,144,384]{2,1,0:T(8,128)(2,1)S(1)} collective-permute-done((bf16[1,144,384]{2,1,0:T(8,128)(2,1)}, bf16[1,144,384]{2,1,0:T(8,128)(2,1)S(1)}, u32[]{:S(2)}, u32[]{:S(2)}) %collective-permute-start.6) | collective-permute-done | bytes 110624 | tf_op jit(solution)/shard_map/ppermute | solution.py:657
  52.8 1.9 join.5
  57.6 3.3 place_blocks.2
  66.3 1.9 join.7.refs_4_
  69.4 1.7 join.6.refs_0_
  73.1 9.7 %attn_fwd.2 = (bf16[1024,2304]{1,0:T(8,128)(2,1)}, bf16[1024,768]{1,0:T(8,128)(2,1)}, bf16[2,12,512,512]{3,2,1,0:T(8,128)(2,1)}) custom-call(bf16[1024,768]{1,0:T(8,128)(2,1)} %bitcast.252, bf16[768,768]{1,0:T(8,128)(2,1)} %copy-done.7, f32[1,2304]{1,0:T(1,128)} %reshape.639.b_ref, f32[6,8,1024]{2,1,0:T(8,128)} %pad.46.dist_ref, f32[2,8,512]{2,1,0:T(8,128)} %pad.43.mask_ref), custom_call_target="tpu_custom_call" | custom-call | flops 1150000 | tf_op jit(solution)/shard_map/attn_fwd/pallas_call | solution.py:155
  85.4 1.5 collective-permute-done.13.refs_2_
  87.4 3.3 place_blocks.3
  93.1 17.2 %attn_fwd.3 = (bf16[1024,2304]{1,0:T(8,128)(2,1)}, bf16[1024,768]{1,0:T(8,128)(2,1)}, bf16[2,12,512,512]{3,2,1,0:T(8,128)(2,1)}) custom-call(bf16[1024,768]{1,0:T(8,128)(2,1)} %bitcast.253, bf16[768,1536]{1,0:T(8,128)(2,1)} %copy-done.3, f32[1,2304]{1,0:T(1,128)} %reshape.639.b_ref, ...), custom_call_target="tpu_custom_call", output_to_operand_aliasing={{0}: (5, {}), {1}: (6, {}), {2}: (7, {})} | custom-call | flops 1150000 | tf_op jit(solution)/shard_map/attn_fwd/pallas_call | solution.py:155
  110.3 29.6 %ffn_in.1 = (f32[1024,768]{1,0:T(8,128)}, f32[1024,1]{1,0:T(8,128)}, bf16[1024,768]{1,0:T(8,128)(2,1)}, bf16[1024,3072]{1,0:T(8,128)(2,1)}, bf16[1024,3072]{1,0:T(8,128)(2,1)}) custom-call(bf16[1024,768]{1,0:T(8,128)(2,1)} %bitcast.254, bf16[1024,768]{1,0:T(8,128)(2,1)} %get-tuple-element.190.ctx_ref.o_ref, bf16[768,768]{1,0:T(8,128)(2,1)} %copy-done.2, ...), custom_call_target="tpu_custom_call" | custom-call | flops 1150000 | tf_op jit(solution)/shard_map/ffn_in/pallas_call | solution.py:331
  139.9 9.9 %all-gather.5.cloned.1.call-done.w_ref.w2_ref = bf16[3072,768]{1,0:T(8,128)(2,1)} async-done(((bf16[96,768]{1,0:T(8,128)(2,1)}), bf16[3072,768]{1,0:T(8,128)(2,1)}) %all-gather.5.cloned.1.call-update) | async-done | bytes 4718608 | tf_op jit(solution)/shard_map/all_gather | solution.py:997
  149.9 11.2 %ffn_out.1 = (f32[1024,768]{1,0:T(8,128)}, f32[1024,1]{1,0:T(8,128)}, bf16[1024,768]{1,0:T(8,128)(2,1)}, f32[4,8,128]{2,1,0:T(8,128)}) custom-call(bf16[1024,3072]{1,0:T(8,128)(2,1)} %get-tuple-element.195.act_ref, bf16[3072,768]{1,0:T(8,128)(2,1)} %all-gather.5.cloned.1.call-done.w_ref.w2_ref, f32[1024,768]{1,0:T(8,128)} %get-tuple-element.197.n1_ref, ...), custom_call_target="tpu_custom_call" | custom-call | flops 1150000 | tf_op jit(solution)/shard_map/ffn_out/pallas_call | solution.py:373
  162.0 5.3 %all_gather.11 = f32[2,4,2]{2,0,1:T(2,128)S(1)} all-gather(f32[2,1,2]{2,0,1:T(2,128)S(1)} %reshape_squeeze.20), channel_id=1, replica_groups=mesh['query'=8,'cand'=4] {'cand'}, dimensions={1}, use_global_device_ids=true | all-gather | bytes 80 | tf_op jit(solution)/shard_map/all_gather | solution.py:1079
  167.9 16.4 %outer_bwd.1 = (f32[1024,768]{1,0:T(8,128)}, bf16[1024,768]{1,0:T(8,128)(2,1)}, f32[8,768]{1,0:T(8,128)}, f32[2,128]{1,0:T(2,128)}, bf16[4,4,96,768]{3,2,1,0:T(8,128)(2,1)}, /*index=5*/bf16[4,4,96,768]{3,2,1,0:T(8,128)(2,1)}) custom-call(s32[5]{0:T(128)} %stack.61.place_ref.spot_ref, f32[2,8]{1,0:T(2,128)} %reshape.641.score_ref, s32[2,8]{1,0:T(2,128)} %reshape.636.len_ref, ...), custom_call_target="tpu_custom_call" | custom-call | flops 1150000 | tf_op jit(solution)/shard_map/outer_bwd/pallas_call | solution.py:475
  184.5 11.7 %act_bwd.1 = (bf16[1024,3072]{1,0:T(8,128)(2,1)}, f32[1,3072]{1,0:T(1,128)}) custom-call(bf16[1024,768]{1,0:T(8,128)(2,1)} %get-tuple-element.205.dr_ref, bf16[1024,3072]{1,0:T(8,128)(2,1)} %get-tuple-element.206.slope_ref, bf16[3072,768]{1,0:T(8,128)(2,1)} %all-gather.5.cloned.1.call-done.w_ref.w2_ref), custom_call_target="tpu_custom_call" | custom-call | flops 1150000 | tf_op jit(solution)/shard_map/act_bwd/pallas_call | solution.py:525
  196.3 1.9 fusion.2
  199.4 24.3 %inner_bwd.1 = (f32[1024,768]{1,0:T(8,128)}, bf16[1024,768]{1,0:T(8,128)(2,1)}, f32[8,768]{1,0:T(8,128)}, bf16[384,3840]{1,0:T(8,128)(2,1)}, bf16[384,3840]{1,0:T(8,128)(2,1)}) custom-call(s32[5]{0:T(128)} %stack.61.place_ref.spot_ref, bf16[1024,3072]{1,0:T(8,128)(2,1)} %get-tuple-element.210.din_ref, ...), custom_call_target="tpu_custom_call" | custom-call | flops 1150000 | tf_op jit(solution)/shard_map/inner_bwd/pallas_call | solution.py:599
  223.7 2.0 collective-permute-done.18
  226.8 1.6 fusion.3
  229.7 15.2 %attn_bwd.2 = (bf16[1024,768]{1,0:T(8,128)(2,1)}, f32[2,8,1024]{2,1,0:T(8,128)}, f32[2,8,384]{2,1,0:T(8,128)}, bf16[384,768]{1,0:T(8,128)(2,1)}, bf16[384,768]{1,0:T(8,128)(2,1)}) custom-call(s32[5]{0:T(128)} %stack.61.place_ref.spot_ref, bf16[1024,2304]{1,0:T(8,128)(2,1)} %get-tuple-element.199.qkv_ref, bf16[1024,768]{1,0:T(8,128)(2,1)} %get-tuple-element.190.ctx_ref.o_ref, ...), custom_call_target="tpu_custom_call" | custom-call | flops 1150000 | tf_op jit(solution)/shard_map/attn_bwd/pallas_call | solution.py:250
  244.9 3.5 fusion
  249.3 1.6 collective-permute-done.21
  252.8 1.6 fusion.23
  256.5 27.2 %attn_bwd.3 = (bf16[1024,1536]{1,0:T(8,128)(2,1)}, f32[4,8,1024]{2,1,0:T(8,128)}, f32[4,8,384]{2,1,0:T(8,128)}, bf16[384,1536]{1,0:T(8,128)(2,1)}, bf16[384,1536]{1,0:T(8,128)(2,1)}) custom-call(s32[5]{0:T(128)} %stack.61.place_ref.spot_ref, bf16[1024,2304]{1,0:T(8,128)(2,1)} %get-tuple-element.199.qkv_ref, ...), custom_call_target="tpu_custom_call" | custom-call | flops 1150000 | tf_op jit(solution)/shard_map/attn_bwd/pallas_call | solution.py:250
  284.5 1.5 collective-permute-start.27
  289.9 1.8 fusion.1
  298.7 4.3 %add_add_fusion = f32[1024,768]{1,0:T(8,128)} fusion(f32[1024,768]{1,0:T(8,128)S(1)} %copy-done.42, f32[1024,768]{1,0:T(8,128)S(1)} %fusion.62, bf16[1024,1536]{1,0:T(8,128)(2,1)S(1)} %copy-done.43, bf16[768,1536]{1,0:T(8,128)(2,1)S(1)} %copy-done.4), kind=kOutput, calls=%fused_computation | convolution fusion | flops 2417491968 | bytes 14942208 | tf_op jit(solution)/shard_map/dot_general | solution.py:53
  303.0 6.9 %collective-permute-done.31 = bf16[4,24,3840]{2,1,0:T(8,128)(2,1)S(1)} collective-permute-done((bf16[4,24,3840]{2,1,0:T(8,128)(2,1)S(1)}, bf16[4,24,3840]{2,1,0:T(8,128)(2,1)S(1)}, u32[]{:S(2)}, u32[]{:S(2)}) %collective-permute-start.31) | collective-permute-done | bytes 737312 | tf_op jit(solution)/shard_map/ppermute | solution.py:657
  309.9 2.3 collective-permute-done.29
  312.2 2.5 fusion.11
  314.7 1.6 collective-permute-start.37
  316.3 2.7 collective-permute-start.38
  320.7 2.0 fusion.21
  324.4 7.4 %collective-permute-done.38 = bf16[24,3840]{1,0:T(8,128)(2,1)} collective-permute-done((bf16[24,3840]{1,0:T(8,128)(2,1)}, bf16[24,3840]{1,0:T(8,128)(2,1)}, u32[]{:S(2)}, u32[]{:S(2)}) %collective-permute-start.38) | collective-permute-done | bytes 184352 | tf_op jit(solution)/shard_map/ppermute | solution.py:657
  331.7 2.9 collective-permute-done.39
  337.6 1.6 fusion.16
  340.6 9.9 %collective-permute-done.35 = bf16[40,2304]{1,0:T(8,128)(2,1)S(1)} collective-permute-done((bf16[40,2304]{1,0:T(8,128)(2,1)S(1)}, bf16[40,2304]{1,0:T(8,128)(2,1)S(1)}, u32[]{:S(2)}, u32[]{:S(2)}) %collective-permute-start.35) | collective-permute-done | bytes 184352 | tf_op jit(solution)/shard_map/ppermute | solution.py:657
  350.5 2.5 collective-permute-done.36
  (256 shorter events, 67.8 us)
Async XLA Ops:
  7.2 45.3 %copy-start.41 = (s32[1023]{0:T(1024)S(1)}, s32[1023]{0:T(1024)}, u32[]{:S(2)}) copy-start(s32[1023]{0:T(1024)} %param.26) | copy-start | bytes 12280
  7.2 103.1 %all-gather.3.cloned.1.call-start = ((), (), s32[]{:S(2)}) async-start(), calls=%async_computation | async-start | bytes 4866048 | tf_op jit(solution)/shard_map/all_gather | solution.py:996
  8.9 140.9 %all-gather.5.cloned.1.call-start = ((), (), s32[]{:S(2)}) async-start(), calls=%async_computation.1 | async-start | bytes 4866048 | tf_op jit(solution)/shard_map/all_gather | solution.py:997
  17.6 8.7 %collective-permute-start = (bf16[1,64,768]{2,1,0:T(8,128)(2,1)}, bf16[1,64,768]{2,1,0:T(8,128)(2,1)S(1)}, u32[]{:S(2)}, u32[]{:S(2)}) collective-permute-start(bf16[1,64,768]{2,1,0:T(8,128)(2,1)} %bitcast.295), channel_id=1, source_target_pairs={{0,8},{4,12},{8,16},{12,20},{16,24},{20,28},{24,0},{28,4},{1,9},{5... | collective-permute-start | bytes 294920 | tf_op jit(solution)/shard_map/ppermute | solution.py:657
  18.9 9.2 %collective-permute-start.1 = (bf16[1,64,768]{2,1,0:T(8,128)(2,1)}, bf16[1,64,768]{2,1,0:T(8,128)(2,1)S(1)}, u32[]{:S(2)}, u32[]{:S(2)}) collective-permute-start(bf16[1,64,768]{2,1,0:T(8,128)(2,1)} %bitcast.296), channel_id=1, source_target_pairs={{0,16},{4,20},{8,24},{12,28},{16,0},{20,4},{24,8},{28,12},{1,17},{... | collective-permute-start | bytes 294920 | tf_op jit(solution)/shard_map/ppermute | solution.py:657
  19.9 11.7 %collective-permute-start.2 = (bf16[1,64,768]{2,1,0:T(8,128)(2,1)}, bf16[1,64,768]{2,1,0:T(8,128)(2,1)S(1)}, u32[]{:S(2)}, u32[]{:S(2)}) collective-permute-start(bf16[1,64,768]{2,1,0:T(8,128)(2,1)} %bitcast.297), channel_id=1, source_target_pairs={{0,24},{4,28},{8,0},{12,4},{16,8},{20,12},{24,16},{28,20},{1,25},{... | collective-permute-start | bytes 294920 | tf_op jit(solution)/shard_map/ppermute | solution.py:657
  34.1 17.8 %collective-permute-start.3 = (bf16[4,64,768]{2,1,0:T(8,128)(2,1)}, bf16[4,64,768]{2,1,0:T(8,128)(2,1)S(1)}, u32[]{:S(2)}, u32[]{:S(2)}) collective-permute-start(bf16[4,64,768]{2,1,0:T(8,128)(2,1)} %join.4.refs_0_), channel_id=1, source_target_pairs={{0,4},{4,0},{8,12},{12,8},{16,20},{20,16},{24,28},{28,24},{1,5},{5... | collective-permute-start | bytes 1179656 | tf_op jit(solution)/shard_map/ppermute | solution.py:657
  35.3 5.5 %collective-permute-start.4 = (bf16[1,144,384]{2,1,0:T(8,128)(2,1)}, bf16[1,144,384]{2,1,0:T(8,128)(2,1)S(1)}, u32[]{:S(2)}, u32[]{:S(2)}) collective-permute-start(bf16[1,144,384]{2,1,0:T(8,128)(2,1)} %bitcast.291), channel_id=1, source_target_pairs={{0,8},{4,12},{8,16},{12,20},{16,24},{20,28},{24,0},{28,4},{1,9},{5... | collective-permute-start | bytes 331784 | tf_op jit(solution)/shard_map/ppermute | solution.py:657
  35.3 7.8 %collective-permute-start.5 = (bf16[1,144,384]{2,1,0:T(8,128)(2,1)}, bf16[1,144,384]{2,1,0:T(8,128)(2,1)S(1)}, u32[]{:S(2)}, u32[]{:S(2)}) collective-permute-start(bf16[1,144,384]{2,1,0:T(8,128)(2,1)} %bitcast.292), channel_id=1, source_target_pairs={{0,16},{4,20},{8,24},{12,28},{16,0},{20,4},{24,8},{28,12},{1,17},{... | collective-permute-start | bytes 331784 | tf_op jit(solution)/shard_map/ppermute | solution.py:657
  37.0 14.9 %collective-permute-start.6 = (bf16[1,144,384]{2,1,0:T(8,128)(2,1)}, bf16[1,144,384]{2,1,0:T(8,128)(2,1)S(1)}, u32[]{:S(2)}, u32[]{:S(2)}) collective-permute-start(bf16[1,144,384]{2,1,0:T(8,128)(2,1)} %bitcast.293), channel_id=1, source_target_pairs={{0,24},{4,28},{8,0},{12,4},{16,8},{20,12},{24,16},{28,20},{1,25},{... | collective-permute-start | bytes 331784 | tf_op jit(solution)/shard_map/ppermute | solution.py:657
  37.5 18.4 %collective-permute-start.7 = (bf16[4,64,768]{2,1,0:T(8,128)(2,1)}, bf16[4,64,768]{2,1,0:T(8,128)(2,1)S(1)}, u32[]{:S(2)}, u32[]{:S(2)}) collective-permute-start(bf16[4,64,768]{2,1,0:T(8,128)(2,1)} %join.4.refs_0_), channel_id=1, source_target_pairs={{0,1},{1,0},{2,3},{3,2},{4,5},{5,4},{6,7},{7,6},{8,9},{9,8},{10,11... | collective-permute-start | bytes 1179656 | tf_op jit(solution)/shard_map/ppermute | solution.py:657
  51.9 4.0 %collective-permute-start.8 = (bf16[4,64,768]{2,1,0:T(8,128)(2,1)S(1)}, bf16[4,64,768]{2,1,0:T(8,128)(2,1)S(1)}, u32[]{:S(2)}, u32[]{:S(2)}) collective-permute-start(bf16[4,64,768]{2,1,0:T(8,128)(2,1)S(1)} %collective-permute-done.3.refs_1_), channel_id=1, source_target_pairs={{0,1},{1,0},{2,3},{3,2},{4,5},{5,4},{6,7},{7,6},{8,9},{9,8},{10,11... | collective-permute-start | bytes 1179656 | tf_op jit(solution)/shard_map/ppermute | solution.py:657
  54.7 10.8 %collective-permute-start.10 = (bf16[4,96,384]{2,1,0:T(8,128)(2,1)}, bf16[4,96,384]{2,1,0:T(8,128)(2,1)S(1)}, u32[]{:S(2)}, u32[]{:S(2)}) collective-permute-start(bf16[4,96,384]{2,1,0:T(8,128)(2,1)} %get-tuple-element.167.refs_0_), channel_id=1, source_target_pairs={{0,2},{1,3},{2,0},{3,1},{4,6},{5,7},{6,4},{7,5},{8,10},{9,11},{10,... | collective-permute-start | bytes 884744 | tf_op jit(solution)/shard_map/ppermute | solution.py:657
  55.5 10.0 %collective-permute-start.9 = (bf16[4,48,384]{2,1,0:T(8,128)(2,1)}, bf16[4,48,384]{2,1,0:T(8,128)(2,1)S(1)}, u32[]{:S(2)}, u32[]{:S(2)}) collective-permute-start(bf16[4,48,384]{2,1,0:T(8,128)(2,1)} %get-tuple-element.161.refs_0_), channel_id=1, source_target_pairs={{0,4},{4,0},{8,12},{12,8},{16,20},{20,16},{24,28},{28,24},{1,5},{5... | collective-permute-start | bytes 442376 | tf_op jit(solution)/shard_map/ppermute | solution.py:657
  68.3 15.6 %collective-permute-start.12 = (bf16[8,96,384]{2,1,0:T(8,128)(2,1)}, bf16[8,96,384]{2,1,0:T(8,128)(2,1)S(1)}, u32[]{:S(2)}, u32[]{:S(2)}) collective-permute-start(bf16[8,96,384]{2,1,0:T(8,128)(2,1)} %join.7.refs_4_), channel_id=1, source_target_pairs={{0,4},{4,0},{8,12},{12,8},{16,20},{20,16},{24,28},{28,24},{1,5},{5... | collective-permute-start | bytes 1769480 | tf_op jit(solution)/shard_map/ppermute | solution.py:657
  71.1 11.8 %collective-permute-start.11 = (bf16[8,48,384]{2,1,0:T(8,128)(2,1)}, bf16[8,48,384]{2,1,0:T(8,128)(2,1)S(1)}, u32[]{:S(2)}, u32[]{:S(2)}) collective-permute-start(bf16[8,48,384]{2,1,0:T(8,128)(2,1)} %join.6.refs_0_), channel_id=1, source_target_pairs={{0,2},{1,3},{2,0},{3,1},{4,6},{5,7},{6,4},{7,5},{8,10},{9,11},{10,... | collective-permute-start | bytes 884744 | tf_op jit(solution)/shard_map/ppermute | solution.py:657
  71.7 15.2 %collective-permute-start.15 = (bf16[8,96,384]{2,1,0:T(8,128)(2,1)}, bf16[8,96,384]{2,1,0:T(8,128)(2,1)}, u32[]{:S(2)}, u32[]{:S(2)}) collective-permute-start(bf16[8,96,384]{2,1,0:T(8,128)(2,1)} %join.7.refs_4_), channel_id=1, source_target_pairs={{0,1},{1,0},{2,3},{3,2},{4,5},{5,4},{6,7},{7,6},{8,9},{9,8},{10,11... | collective-permute-start | bytes 1769480 | tf_op jit(solution)/shard_map/ppermute | solution.py:657
  83.8 3.6 collective-permute-start.16
  84.9 2.0 collective-permute-start.13
  84.9 2.5 collective-permute-start.14
  184.3 11.9 %collective-permute-start.17 = (bf16[4,4,96,768]{3,2,1,0:T(8,128)(2,1)}, bf16[4,4,96,768]{3,2,1,0:T(8,128)(2,1)}, u32[]{:S(2)}, u32[]{:S(2)}) collective-permute-start(bf16[4,4,96,768]{3,2,1,0:T(8,128)(2,1)} %get-tuple-element.209), channel_id=1, source_target_pairs={{0,1},{1,0},{2,3},{3,2},{4,5},{5,4},{6,7},{7,6},{8,9},{9,8},{10,11... | collective-permute-start | bytes 7077896 | tf_op jit(solution)/shard_map/ppermute | solution.py:657
  198.2 27.4 %collective-permute-start.18 = (bf16[2,4,96,768]{3,2,1,0:T(8,128)(2,1)S(1)}, bf16[2,4,96,768]{3,2,1,0:T(8,128)(2,1)}, u32[]{:S(2)}, u32[]{:S(2)}) collective-permute-start(bf16[2,4,96,768]{3,2,1,0:T(8,128)(2,1)S(1)} %fusion.2), channel_id=1, source_target_pairs={{0,2},{1,3},{2,0},{3,1},{4,6},{5,7},{6,4},{7,5},{8,10},{9,11},{10,... | collective-permute-start | bytes 3538952 | tf_op jit(solution)/shard_map/ppermute | solution.py:657
  225.6 19.3 %collective-permute-start.20 = (bf16[384,3840]{1,0:T(8,128)(2,1)}, bf16[384,3840]{1,0:T(8,128)(2,1)}, u32[]{:S(2)}, u32[]{:S(2)}) collective-permute-start(bf16[384,3840]{1,0:T(8,128)(2,1)} %get-tuple-element.229), channel_id=1, source_target_pairs={{0,1},{1,0},{2,3},{3,2},{4,5},{5,4},{6,7},{7,6},{8,9},{9,8},{10,11... | collective-permute-start | bytes 8847368 | tf_op jit(solution)/shard_map/ppermute | solution.py:657
  228.4 16.5 %collective-permute-start.19 = (bf16[4,96,768]{2,1,0:T(8,128)(2,1)S(1)}, bf16[4,96,768]{2,1,0:T(8,128)(2,1)S(1)}, u32[]{:S(2)}, u32[]{:S(2)}) collective-permute-start(bf16[4,96,768]{2,1,0:T(8,128)(2,1)S(1)} %fusion.3), channel_id=1, source_target_pairs={{0,4},{4,0},{8,12},{12,8},{16,20},{20,16},{24,28},{28,24},{1,5},{5... | collective-permute-start | bytes 1769480 | tf_op jit(solution)/shard_map/ppermute | solution.py:657
  248.4 35.4 %collective-permute-start.26 = (bf16[2,4,24,3840]{3,2,1,0:T(8,128)(2,1)}, bf16[2,4,24,3840]{3,2,1,0:T(8,128)(2,1)}, u32[]{:S(2)}, u32[]{:S(2)}) collective-permute-start(bf16[2,4,24,3840]{3,2,1,0:T(8,128)(2,1)} %fusion), channel_id=1, source_target_pairs={{0,4},{4,0},{8,12},{12,8},{16,20},{20,16},{24,28},{28,24},{1,5},{5... | collective-permute-start | bytes 4423688 | tf_op jit(solution)/shard_map/ppermute | solution.py:657
  248.7 2.2 collective-permute-start.21
  251.7 32.1 %collective-permute-start.22 = (bf16[2,4,24,768]{3,2,1,0:T(8,128)(2,1)S(1)}, bf16[2,4,24,768]{3,2,1,0:T(8,128)(2,1)S(1)}, u32[]{:S(2)}, u32[]{:S(2)}) collective-permute-start(bf16[2,4,24,768]{3,2,1,0:T(8,128)(2,1)S(1)} %fusion.18), channel_id=1, source_target_pairs={{0,2},{1,3},{2,0},{3,1},{4,6},{5,7},{6,4},{7,5},{8,10},{9,11},{10,... | collective-permute-start | bytes 884744 | tf_op jit(solution)/shard_map/ppermute | solution.py:657
  254.4 29.3 %collective-permute-start.23 = (bf16[96,768]{1,0:T(8,128)(2,1)S(1)}, bf16[96,768]{1,0:T(8,128)(2,1)S(1)}, u32[]{:S(2)}, u32[]{:S(2)}) collective-permute-start(bf16[96,768]{1,0:T(8,128)(2,1)S(1)} %get-tuple-element.352), channel_id=1, source_target_pairs={{0,8},{4,12},{8,16},{12,20},{16,24},{20,28},{24,0},{28,4},{1,9},{5... | collective-permute-start | bytes 442376 | tf_op jit(solution)/shard_map/ppermute | solution.py:657
  255.0 28.7 %collective-permute-start.24 = (bf16[96,768]{1,0:T(8,128)(2,1)S(1)}, bf16[96,768]{1,0:T(8,128)(2,1)S(1)}, u32[]{:S(2)}, u32[]{:S(2)}) collective-permute-start(bf16[96,768]{1,0:T(8,128)(2,1)S(1)} %get-tuple-element.351), channel_id=1, source_target_pairs={{0,16},{4,20},{8,24},{12,28},{16,0},{20,4},{24,8},{28,12},{1,17},{... | collective-permute-start | bytes 442376 | tf_op jit(solution)/shard_map/ppermute | solution.py:657
  256.5 27.3 %collective-permute-start.25 = (bf16[96,768]{1,0:T(8,128)(2,1)S(1)}, bf16[96,768]{1,0:T(8,128)(2,1)S(1)}, u32[]{:S(2)}, u32[]{:S(2)}) collective-permute-start(bf16[96,768]{1,0:T(8,128)(2,1)S(1)} %get-tuple-element.350), channel_id=1, source_target_pairs={{0,24},{4,28},{8,0},{12,4},{16,8},{20,12},{24,16},{28,20},{1,25},{... | collective-permute-start | bytes 442376 | tf_op jit(solution)/shard_map/ppermute | solution.py:657
  256.5 30.4 %copy-start.37 = (f32[2,8,384]{2,1,0:T(8,128)S(1)}, f32[2,8,384]{2,1,0:T(8,128)}, u32[]{:S(2)}) copy-start(f32[2,8,384]{2,1,0:T(8,128)} %get-tuple-element.256) | copy-start | bytes 73732
  256.5 31.3 %copy-start.13 = (pred[1023,256]{1,0:T(8,128)(4,1)S(1)}, pred[1023,256]{1,0:T(8,128)(4,1)}, u32[]{:S(2)}) copy-start(pred[1023,256]{1,0:T(8,128)(4,1)} %copy-done.12) | copy-start | bytes 785668
  256.5 32.3 %copy-start.38 = (f32[1,3072]{1,0:T(1,128)S(1)}, f32[1,3072]{1,0:T(1,128)}, u32[]{:S(2)}) copy-start(f32[1,3072]{1,0:T(1,128)} %get-tuple-element.258) | copy-start | bytes 36868
  256.5 33.0 %copy-start.40 = (f32[8,768]{1,0:T(8,128)S(1)}, f32[8,768]{1,0:T(8,128)}, u32[]{:S(2)}) copy-start(f32[8,768]{1,0:T(8,128)} %get-tuple-element.254) | copy-start | bytes 73732
  256.5 33.0 %copy-start.39 = (f32[8,768]{1,0:T(8,128)S(1)}, f32[8,768]{1,0:T(8,128)}, u32[]{:S(2)}) copy-start(f32[8,768]{1,0:T(8,128)} %get-tuple-element.255) | copy-start | bytes 73732
  284.5 9.9 %collective-permute-start.27 = (bf16[384,1536]{1,0:T(8,128)(2,1)}, bf16[384,1536]{1,0:T(8,128)(2,1)S(1)}, u32[]{:S(2)}, u32[]{:S(2)}) collective-permute-start(bf16[384,1536]{1,0:T(8,128)(2,1)} %get-tuple-element.261), channel_id=1, source_target_pairs={{0,1},{1,0},{2,3},{3,2},{4,5},{5,4},{6,7},{7,6},{8,9},{9,8},{10,11... | collective-permute-start | bytes 3538952 | tf_op jit(solution)/shard_map/ppermute | solution.py:657
  291.7 18.2 %collective-permute-start.31 = (bf16[4,24,3840]{2,1,0:T(8,128)(2,1)S(1)}, bf16[4,24,3840]{2,1,0:T(8,128)(2,1)S(1)}, u32[]{:S(2)}, u32[]{:S(2)}) collective-permute-start(bf16[4,24,3840]{2,1,0:T(8,128)(2,1)S(1)} %fusion.1), channel_id=1, source_target_pairs={{0,2},{1,3},{2,0},{3,1},{4,6},{5,7},{6,4},{7,5},{8,10},{9,11},{10,... | collective-permute-start | bytes 2211848 | tf_op jit(solution)/shard_map/ppermute | solution.py:657
  293.3 9.7 %collective-permute-start.30 = (bf16[4,24,768]{2,1,0:T(8,128)(2,1)S(1)}, bf16[4,24,768]{2,1,0:T(8,128)(2,1)S(1)}, u32[]{:S(2)}, u32[]{:S(2)}) collective-permute-start(bf16[4,24,768]{2,1,0:T(8,128)(2,1)S(1)} %fusion.22), channel_id=1, source_target_pairs={{0,4},{4,0},{8,12},{12,8},{16,20},{20,16},{24,28},{28,24},{1,5},{5... | collective-permute-start | bytes 442376 | tf_op jit(solution)/shard_map/ppermute | solution.py:657
  294.7 24.4 %collective-permute-start.32 = (bf16[2,4,24,1536]{3,2,1,0:T(8,128)(2,1)S(1)}, bf16[2,4,24,1536]{3,2,1,0:T(8,128)(2,1)S(1)}, u32[]{:S(2)}, u32[]{:S(2)}) collective-permute-start(bf16[2,4,24,1536]{3,2,1,0:T(8,128)(2,1)S(1)} %fusion.9), channel_id=1, source_target_pairs={{0,4},{4,0},{8,12},{12,8},{16,20},{20,16},{24,28},{28,24},{1,5},{5... | collective-permute-start | bytes 1769480 | tf_op jit(solution)/shard_map/ppermute | solution.py:657
  295.2 2.3 collective-permute-start.28
  297.6 14.6 %collective-permute-start.29 = (bf16[16,1536]{1,0:T(8,128)(2,1)S(1)}, bf16[16,1536]{1,0:T(8,128)(2,1)S(1)}, u32[]{:S(2)}, u32[]{:S(2)}) collective-permute-start(bf16[16,1536]{1,0:T(8,128)(2,1)S(1)} %fusion.41), channel_id=1, source_target_pairs={{0,4},{4,0},{8,12},{12,8},{16,20},{20,16},{24,28},{28,24},{1,5},{5... | collective-permute-start | bytes 147464 | tf_op jit(solution)/shard_map/ppermute | solution.py:657
  314.7 9.6 %collective-permute-start.37 = (bf16[24,3840]{1,0:T(8,128)(2,1)}, bf16[24,3840]{1,0:T(8,128)(2,1)}, u32[]{:S(2)}, u32[]{:S(2)}) collective-permute-start(bf16[24,3840]{1,0:T(8,128)(2,1)} %get-tuple-element.349), channel_id=1, source_target_pairs={{0,8},{4,12},{8,16},{12,20},{16,24},{20,28},{24,0},{28,4},{1,9},{5... | collective-permute-start | bytes 552968 | tf_op jit(solution)/shard_map/ppermute | solution.py:657
  316.3 15.4 %collective-permute-start.38 = (bf16[24,3840]{1,0:T(8,128)(2,1)}, bf16[24,3840]{1,0:T(8,128)(2,1)}, u32[]{:S(2)}, u32[]{:S(2)}) collective-permute-start(bf16[24,3840]{1,0:T(8,128)(2,1)} %get-tuple-element.348), channel_id=1, source_target_pairs={{0,16},{4,20},{8,24},{12,28},{16,0},{20,4},{24,8},{28,12},{1,17},{... | collective-permute-start | bytes 552968 | tf_op jit(solution)/shard_map/ppermute | solution.py:657
  319.0 15.6 %collective-permute-start.39 = (bf16[24,3840]{1,0:T(8,128)(2,1)}, bf16[24,3840]{1,0:T(8,128)(2,1)}, u32[]{:S(2)}, u32[]{:S(2)}) collective-permute-start(bf16[24,3840]{1,0:T(8,128)(2,1)} %get-tuple-element.347), channel_id=1, source_target_pairs={{0,24},{4,28},{8,0},{12,4},{16,8},{20,12},{24,16},{28,20},{1,25},{... | collective-permute-start | bytes 552968 | tf_op jit(solution)/shard_map/ppermute | solution.py:657
  319.9 14.7 %collective-permute-start.33 = (bf16[112,1536]{1,0:T(8,128)(2,1)S(1)}, bf16[112,1536]{1,0:T(8,128)(2,1)S(1)}, u32[]{:S(2)}, u32[]{:S(2)}) collective-permute-start(bf16[112,1536]{1,0:T(8,128)(2,1)S(1)} %pad_maximum_fusion), channel_id=1, source_target_pairs={{0,2},{1,3},{2,0},{3,1},{4,6},{5,7},{6,4},{7,5},{8,10},{9,11},{10,... | collective-permute-start | bytes 1032200 | tf_op jit(solution)/shard_map/ppermute | solution.py:657
  335.8 4.8 %collective-permute-start.34 = (bf16[40,2304]{1,0:T(8,128)(2,1)S(1)}, bf16[40,2304]{1,0:T(8,128)(2,1)S(1)}, u32[]{:S(2)}, u32[]{:S(2)}) collective-permute-start(bf16[40,2304]{1,0:T(8,128)(2,1)S(1)} %get-tuple-element.364), channel_id=1, source_target_pairs={{0,8},{4,12},{8,16},{12,20},{16,24},{20,28},{24,0},{28,4},{1,9},{5... | collective-permute-start | bytes 552968 | tf_op jit(solution)/shard_map/ppermute | solution.py:657
  335.9 14.7 %collective-permute-start.35 = (bf16[40,2304]{1,0:T(8,128)(2,1)S(1)}, bf16[40,2304]{1,0:T(8,128)(2,1)S(1)}, u32[]{:S(2)}, u32[]{:S(2)}) collective-permute-start(bf16[40,2304]{1,0:T(8,128)(2,1)S(1)} %get-tuple-element.365), channel_id=1, source_target_pairs={{0,16},{4,20},{8,24},{12,28},{16,0},{20,4},{24,8},{28,12},{1,17},{... | collective-permute-start | bytes 552968 | tf_op jit(solution)/shard_map/ppermute | solution.py:657
  336.2 16.9 %collective-permute-start.36 = (bf16[40,2304]{1,0:T(8,128)(2,1)S(1)}, bf16[40,2304]{1,0:T(8,128)(2,1)S(1)}, u32[]{:S(2)}, u32[]{:S(2)}) collective-permute-start(bf16[40,2304]{1,0:T(8,128)(2,1)S(1)} %get-tuple-element.363), channel_id=1, source_target_pairs={{0,24},{4,28},{8,0},{12,4},{16,8},{20,12},{24,16},{28,20},{1,25},{... | collective-permute-start | bytes 552968 | tf_op jit(solution)/shard_map/ppermute | solution.py:657
  (41 other events, 305.5 us)
Sparse Core Ops, SparseCore 0:
  11.0 72.1 all-gather.2
  86.1 63.7 all-gather.4
where the time goes:
time: 368 us; the launch traced here: 366 us
  Pallas kernels  179 us (49%)
  waiting for transfers between devices  64.9 us (18%)
  starting transfers between devices  37.2 us (10%)
  local copies, waits for them, and re-layouts  32.5 us (9%)
  other arithmetic  26.2 us (7%)
  between operations  14.9 us (4%)
  matrix products  6.46 us (2%)
  blocking collectives  5.29 us (1%)
    ppermute x40, waiting for transfers between devices, move(): lax.ppermute(value, axis, shifted(self.lengths[axis], self.sizes[dim], st...  54.9 us
    pallas_call x2, Pallas kernels, attn_bwd(): pl.pallas_call(partial(attn_bwd_kernel, blocks), grid_spec=pltpu.Prefetch...  42.4 us
    ppermute x40, starting transfers between devices, move(): lax.ppermute(value, axis, shifted(self.lengths[axis], self.sizes[dim], st...  37.1 us
    pallas_call x1, Pallas kernels, ffn_in(): pl.pallas_call(ffn_in_kernel, grid=(hidden // size,), in_specs=[whole, wh...  29.6 us
    pallas_call x2, Pallas kernels, attn_fwd(): pl.pallas_call(attn_fwd_kernel, grid=(pairs, micros), in_specs=[pl.BlockS...  27 us
    pallas_call x1, Pallas kernels, inner_bwd(): pl.pallas_call(partial(inner_bwd_kernel, blocks), grid_spec=pltpu.Prefetc...  24.3 us
    convert_element_type x12, other arithmetic, step(): sent.append(total.astype(BF))  16.6 us
    pallas_call x1, Pallas kernels, outer_bwd(): pl.pallas_call(partial(outer_bwd_kernel, blocks), grid_spec=pltpu.Prefetc...  16.4 us
  transfers between devices with their start and end apart: 42, of which 17 were waited for; matrix products, arithmetic and copies ran while one was open for 11% of the time, Pallas kernels for 41%

commit v1 on v0

--- a/solution.py
+++ b/solution.py
@@ -543,10 +543,22 @@
 
 def inner_bwd_kernel(
     blocks, place_ref, din_ref, w1_ref, low_ref, dr_ref, n1_ref, i1_ref, vec_ref, ctx_ref,
-    one_ref, grad_ref, sum_ref, keep_ref, send_ref, acc, tile, kept, sent,
+    one_ref, grad_ref, sum_ref, keep_ref, send_ref, acc, tile, kept, sent, dr_buf, n1_buf, ctx_buf, sems,
 ):
     step_id = pl.program_id(0)
     last = pl.num_programs(0) - 1
+    needed = [
+        pltpu.make_async_copy(source, buffer, sems.at[index])
+        for index, (source, buffer) in enumerate(
+            ((dr_ref, dr_buf), (n1_ref, n1_buf), (ctx_ref, ctx_buf))
+        )
+    ]
+
+    @pl.when(step_id == 0)
+    def _():
+        for copy in needed:
+            copy.start()
+
     rows = low_ref.shape[0]
 
     @pl.when(step_id < last)
@@ -557,7 +569,7 @@
 
         @pl.when(step_id == 0)
         def _():
-            acc[...] = dr_ref[...] + part
+            acc[...] = part
 
         @pl.when(step_id > 0)
         def _():
@@ -565,12 +577,14 @@
 
     @pl.when(step_id == last)
     def _():
+        for copy in needed:
+            copy.wait()
         sum_ref[...] = jnp.zeros_like(sum_ref)
         gain = vec(vec_ref, "gain_attn")
 
         def step(at):
-            grad_out = acc[at, :]
-            normed = n1_ref[at, :]
+            grad_out = acc[at, :] + dr_buf[at, :]
+            normed = n1_buf[at, :]
             grad_in = norm_backward(grad_out, normed, i1_ref[at, :], gain)
             one_ref[at, :] = grad_in
             grad_low = grad_in.astype(BF)
@@ -580,7 +594,7 @@
             sum_ref[2:3, :] += jnp.sum(grad_low.astype(F32), axis=0, keepdims=True)
 
         row_chunks(rows, 128, step)
-        tile[...] = contract(ctx_ref[...], grad_ref[...], 0, 0)
+        tile[...] = contract(ctx_buf[...], grad_ref[...], 0, 0)
 
     split_rows(place_ref[3], tile, *blocks, kept, sent)
     keep_ref[...] = kept[...].astype(BF)
@@ -596,14 +610,15 @@
     whole = at((rows, width), lambda n: (0, 0))
     near = lambda n: (0, jnp.minimum(n, tiles - 1))
     half = at((width // 2, size), lambda n: (0, n))
+    later = pl.BlockSpec(memory_space=pl.ANY)
     return pl.pallas_call(
         partial(inner_bwd_kernel, blocks),
         grid_spec=pltpu.PrefetchScalarGridSpec(
             num_scalar_prefetch=1,
             grid=(tiles + 1,),
             in_specs=[
-                at((rows, size), near), at((width, size), near), whole, whole, whole,
-                at((rows, 1), lambda n: (0, 0)), at((TABLE_ROWS, width), lambda n: (0, 0)), whole,
+                at((rows, size), near), at((width, size), near), whole, later, later,
+                at((rows, 1), lambda n: (0, 0)), at((TABLE_ROWS, width), lambda n: (0, 0)), later,
             ],
             out_specs=[whole, whole, at((8, width), lambda n: (0, 0)), half, half],
             scratch_shapes=[
@@ -611,6 +626,10 @@
                 pltpu.VMEM((width, size), F32),
                 pltpu.VMEM((width // 2, size), F32),
                 pltpu.VMEM((width // 2, size), F32),
+                pltpu.VMEM((rows, width), F32),
+                pltpu.VMEM((rows, width), F32),
+                pltpu.VMEM((rows, width), BF),
+                pltpu.SemaphoreType.DMA((3,)),
             ],
         ),
         out_shape=[
@@ -994,14 +1013,13 @@
     )
     groups = (group_pairs, pairs - group_pairs)
     w_inner = lax.all_gather(own_part(w_inner), both, axis=0, tiled=True)
-    w_outer = lax.all_gather(own_part(w_outer), both, axis=0, tiled=True)
     stepped = shard % 32 == 0 and width // grid.sizes["far"] == TRIO == PAIR * (pairs // 2)
     if stepped:
         half = shard // 2
         blocks = pack(spot, group_pairs, w_query, w_key, w_value, w_output, table)
         head = Gather(grid, blocks[0][None])
         head.start("outer")
-        lens_row, rel_row, mask = after((lens_row, rel_row, mask), head)
+        lens_row, rel_row, mask, w_outer = after((lens_row, rel_row, mask, w_outer), head)
         (head,) = head.joined()
         block, head.pieces[0] = lax.optimization_barrier((blocks[1], head.pieces[0]))
         rest = Gather(grid, block[None])
@@ -1028,6 +1046,7 @@
         w_output = gather(w_output)
         table = gather(table).reshape(query_size, TABLE_ROWS, width)
 
+    w_outer = lax.all_gather(own_part(w_outer), both, axis=0, tiled=True)
     count = len(VECTORS)
     bias_inner = table[:, count, :inner_shard].reshape(1, hidden).astype(F32)
     rel_bias = table[:, count + 1, : rel_bias.size].reshape(buckets, heads)
@@ -1136,6 +1155,12 @@
     sum_inner.start()
     sum_early.start()
 
+    waiting = (grad_qkv, late_qkv, dist_grad, late_dist, bias_grad, late_bias)
+    waiting = after((*waiting, grad_bias_inner, sums_one, sums_two), sum_late)
+    grad_qkv, late_qkv, dist_grad, late_dist, bias_grad, late_bias = waiting[:6]
+    grad_bias_inner, sums_one, sums_two = waiting[6:]
+    fold = keep.shape[1] // width
+    sum_late.start()
     dist_grad = jnp.concatenate([dist_grad, late_dist])[:, :2].reshape(heads, 2 * length)
     grad_rel = lax.dot_general(
         dist_grad,
@@ -1152,13 +1177,10 @@
         jnp.pad(grad_rel, ((0, 0), (0, width - buckets))),
     ]
     rows = sum(value.shape[0] for value in small)
-    fold = keep.shape[1] // width
     small.append(jnp.zeros((-rows % (8 * fold), width), F32))
     small = jnp.concatenate(small)
     rows = small.shape[0] // fold
     rider = jnp.concatenate([small[i * rows : (i + 1) * rows] for i in range(fold)], axis=1)
-    grad_qkv, late_qkv, rider = after((grad_qkv, late_qkv, rider), sum_late)
-    sum_late.start()
     rider = rider + grid.move(rider.astype(BF), "core", 1).astype(F32)
     other = grid.move(rider.astype(BF), "inner", 1)
     grad_inputs = grad_one + contract(grad_qkv, first_weight, 1, 1)

time: 368 us -> 368 us (level)
  other arithmetic: 26.2 us -> 30.5 us
    convert_element_type x12, other arithmetic: 16.6 us -> 20.8 us  [step(): sent.append(total.astype(BF))]
    unnamed x104 -> x78, local copies, waits for them, and re-layouts: 16 us -> 12.6 us
  transfers between devices with their start and end apart: 42 -> 42, of which waited for: 17 -> 15; matrix products, arithmetic and copies ran while one was open for 11% -> 13% of each run, Pallas kernels for 41% -> 41%
where the time goes in v1:
time: 368 us; the launch traced here: 366 us
  Pallas kernels  177 us (48%)
  waiting for transfers between devices  63.3 us (17%)
  starting transfers between devices  36.1 us (10%)
  local copies, waits for them, and re-layouts  30.8 us (8%)
  other arithmetic  30.5 us (8%)
  between operations  14.8 us (4%)
  matrix products  8.39 us (2%)
  blocking collectives  5.29 us (1%)
    ppermute x40, waiting for transfers between devices, move(): lax.ppermute(value, axis, shifted(self.lengths[axis], self.sizes[dim], st...  51.5 us
    pallas_call x2, Pallas kernels, attn_bwd(): pl.pallas_call(partial(attn_bwd_kernel, blocks), grid_spec=pltpu.Prefetch...  42.3 us
    ppermute x40, starting transfers between devices, move(): lax.ppermute(value, axis, shifted(self.lengths[axis], self.sizes[dim], st...  36 us
    pallas_call x1, Pallas kernels, ffn_in(): pl.pallas_call(ffn_in_kernel, grid=(hidden // size,), in_specs=[whole, wh...  29.5 us
    pallas_call x2, Pallas kernels, attn_fwd(): pl.pallas_call(attn_fwd_kernel, grid=(pairs, micros), in_specs=[pl.BlockS...  27.1 us
    pallas_call x1, Pallas kernels, inner_bwd(): pl.pallas_call(partial(inner_bwd_kernel, blocks), grid_spec=pltpu.Prefetc...  21.9 us
    convert_element_type x12, other arithmetic, step(): sent.append(total.astype(BF))  20.8 us
    pallas_call x1, Pallas kernels, outer_bwd(): pl.pallas_call(partial(outer_bwd_kernel, blocks), grid_spec=pltpu.Prefetc...  16.8 us
  transfers between devices with their start and end apart: 42, of which 15 were waited for; matrix products, arithmetic and copies ran while one was open for 13% of the time, Pallas kernels for 41%

profile of v1, /device:TPU:9, one launch (start us, length us, event | category | flops | bytes accessed | tf_op | source)
XLA Modules:
  0.0 366.2 jit_solution(5568548985773688669)
XLA Ops:
  11.3 1.5 stack.71
  13.5 2.5 pack.1
  18.3 1.5 collective-permute-start.2
  24.6 1.6 collective-permute-done.1.refs_2_
  26.2 3.7 %collective-permute-done.2.refs_3_ = bf16[1,64,768]{2,1,0:T(8,128)(2,1)S(1)} collective-permute-done((bf16[1,64,768]{2,1,0:T(8,128)(2,1)}, bf16[1,64,768]{2,1,0:T(8,128)(2,1)S(1)}, u32[]{:S(2)}, u32[]{:S(2)}) %collective-permute-start.2) | collective-permute-done | bytes 98336 | tf_op jit(solution)/shard_map/ppermute | solution.py:676
  29.9 1.6 constant_dynamic-slice_fusion.1
  31.6 1.8 join.4.refs_0_
  36.1 3.4 collective-permute-start.7
  40.4 10.4 %collective-permute-done.6.refs_3_ = bf16[1,144,384]{2,1,0:T(8,128)(2,1)S(1)} collective-permute-done((bf16[1,144,384]{2,1,0:T(8,128)(2,1)}, bf16[1,144,384]{2,1,0:T(8,128)(2,1)S(1)}, u32[]{:S(2)}, u32[]{:S(2)}) %collective-permute-start.6) | collective-permute-done | bytes 110624 | tf_op jit(solution)/shard_map/ppermute | solution.py:676
  51.6 1.9 join.5
  55.7 3.3 place_blocks.2
  63.7 2.0 join.7.refs_4_
  65.7 1.5 collective-permute-start.12
  67.1 1.7 join.6.refs_0_
  70.5 9.8 %attn_fwd.2 = (bf16[1024,2304]{1,0:T(8,128)(2,1)}, bf16[1024,768]{1,0:T(8,128)(2,1)}, bf16[2,12,512,512]{3,2,1,0:T(8,128)(2,1)}) custom-call(bf16[1024,768]{1,0:T(8,128)(2,1)} %bitcast.252, bf16[768,768]{1,0:T(8,128)(2,1)} %copy-done.7, f32[1,2304]{1,0:T(1,128)} %reshape.639.b_ref, f32[6,8,1024]{2,1,0:T(8,128)} %pad.46.dist_ref, f32[2,8,512]{2,1,0:T(8,128)} %pad.43.mask_ref), custom_call_target="tpu_custom_call" | custom-call | flops 1150000 | tf_op jit(solution)/shard_map/attn_fwd/pallas_call | solution.py:155
  80.4 3.1 collective-permute-done.12.refs_5_
  84.8 1.5 collective-permute-done.13.refs_2_
  86.7 3.3 place_blocks.3
  91.0 1.4 copy-done.3
  92.4 17.3 %attn_fwd.3 = (bf16[1024,2304]{1,0:T(8,128)(2,1)}, bf16[1024,768]{1,0:T(8,128)(2,1)}, bf16[2,12,512,512]{3,2,1,0:T(8,128)(2,1)}) custom-call(bf16[1024,768]{1,0:T(8,128)(2,1)} %bitcast.253, bf16[768,1536]{1,0:T(8,128)(2,1)} %copy-done.3, f32[1,2304]{1,0:T(1,128)} %reshape.639.b_ref, ...), custom_call_target="tpu_custom_call", output_to_operand_aliasing={{0}: (5, {}), {1}: (6, {}), {2}: (7, {})} | custom-call | flops 1150000 | tf_op jit(solution)/shard_map/attn_fwd/pallas_call | solution.py:155
  109.7 29.5 %ffn_in.1 = (f32[1024,768]{1,0:T(8,128)}, f32[1024,1]{1,0:T(8,128)}, bf16[1024,768]{1,0:T(8,128)(2,1)}, bf16[1024,3072]{1,0:T(8,128)(2,1)}, bf16[1024,3072]{1,0:T(8,128)(2,1)}) custom-call(bf16[1024,768]{1,0:T(8,128)(2,1)} %bitcast.254, bf16[1024,768]{1,0:T(8,128)(2,1)} %get-tuple-element.197.ctx_ref.o_ref, bf16[768,768]{1,0:T(8,128)(2,1)} %copy-done.2, ...), custom_call_target="tpu_custom_call" | custom-call | flops 1150000 | tf_op jit(solution)/shard_map/ffn_in/pallas_call | solution.py:331
  139.2 11.8 %all-gather.5.cloned.1.call-done.w_ref.w2_ref = bf16[3072,768]{1,0:T(8,128)(2,1)} async-done(((bf16[96,768]{1,0:T(8,128)(2,1)}), bf16[3072,768]{1,0:T(8,128)(2,1)}) %all-gather.5.cloned.1.call-update) | async-done | bytes 4718608 | tf_op jit(solution)/shard_map/all_gather | solution.py:1049
  151.0 11.2 %ffn_out.1 = (f32[1024,768]{1,0:T(8,128)}, f32[1024,1]{1,0:T(8,128)}, bf16[1024,768]{1,0:T(8,128)(2,1)}, f32[4,8,128]{2,1,0:T(8,128)}) custom-call(bf16[1024,3072]{1,0:T(8,128)(2,1)} %get-tuple-element.203.act_ref, bf16[3072,768]{1,0:T(8,128)(2,1)} %all-gather.5.cloned.1.call-done.w_ref.w2_ref, f32[1024,768]{1,0:T(8,128)} %get-tuple-element.205.n1_ref, ...), custom_call_target="tpu_custom_call" | custom-call | flops 1150000 | tf_op jit(solution)/shard_map/ffn_out/pallas_call | solution.py:373
  163.1 5.3 %all_gather.11 = f32[2,4,2]{2,0,1:T(2,128)S(1)} all-gather(f32[2,1,2]{2,0,1:T(2,128)S(1)} %reshape_squeeze.20), channel_id=1, replica_groups=mesh['query'=8,'cand'=4] {'cand'}, dimensions={1}, use_global_device_ids=true | all-gather | bytes 80 | tf_op jit(solution)/shard_map/all_gather | solution.py:1098
  169.1 16.8 %outer_bwd.1 = (f32[1024,768]{1,0:T(8,128)}, bf16[1024,768]{1,0:T(8,128)(2,1)}, f32[8,768]{1,0:T(8,128)}, f32[2,128]{1,0:T(2,128)}, bf16[4,4,96,768]{3,2,1,0:T(8,128)(2,1)}, /*index=5*/bf16[4,4,96,768]{3,2,1,0:T(8,128)(2,1)}) custom-call(s32[5]{0:T(128)} %stack.61.place_ref.spot_ref, f32[2,8]{1,0:T(2,128)} %reshape.641.score_ref, s32[2,8]{1,0:T(2,128)} %reshape.636.len_ref, ...), custom_call_target="tpu_custom_call" | custom-call | flops 1150000 | tf_op jit(solution)/shard_map/outer_bwd/pallas_call | solution.py:475
  186.0 11.8 %act_bwd.1 = (bf16[1024,3072]{1,0:T(8,128)(2,1)}, f32[1,3072]{1,0:T(1,128)}) custom-call(bf16[1024,768]{1,0:T(8,128)(2,1)} %get-tuple-element.213.dr_ref, bf16[1024,3072]{1,0:T(8,128)(2,1)} %get-tuple-element.214.slope_ref, bf16[3072,768]{1,0:T(8,128)(2,1)} %all-gather.5.cloned.1.call-done.w_ref.w2_ref), custom_call_target="tpu_custom_call" | custom-call | flops 1150000 | tf_op jit(solution)/shard_map/act_bwd/pallas_call | solution.py:525
  197.8 1.9 fusion.2
  200.9 21.9 %inner_bwd.1 = (f32[1024,768]{1,0:T(8,128)}, bf16[1024,768]{1,0:T(8,128)(2,1)}, f32[8,768]{1,0:T(8,128)}, bf16[384,3840]{1,0:T(8,128)(2,1)}, bf16[384,3840]{1,0:T(8,128)(2,1)}) custom-call(s32[5]{0:T(128)} %stack.61.place_ref.spot_ref, bf16[1024,3072]{1,0:T(8,128)(2,1)} %get-tuple-element.218.din_ref, ...), custom_call_target="tpu_custom_call" | custom-call | flops 1150000 | tf_op jit(solution)/shard_map/inner_bwd/pallas_call | solution.py:614
  222.8 4.3 %collective-permute-done.18 = bf16[2,4,96,768]{3,2,1,0:T(8,128)(2,1)} collective-permute-done((bf16[2,4,96,768]{3,2,1,0:T(8,128)(2,1)S(1)}, bf16[2,4,96,768]{3,2,1,0:T(8,128)(2,1)}, u32[]{:S(2)}, u32[]{:S(2)}) %collective-permute-start.18) | collective-permute-done | bytes 1179680 | tf_op jit(solution)/shard_map/ppermute | solution.py:676
  228.2 1.6 fusion.3
  231.1 15.2 %attn_bwd.2 = (bf16[1024,768]{1,0:T(8,128)(2,1)}, f32[2,8,1024]{2,1,0:T(8,128)}, f32[2,8,384]{2,1,0:T(8,128)}, bf16[384,768]{1,0:T(8,128)(2,1)}, bf16[384,768]{1,0:T(8,128)(2,1)}) custom-call(s32[5]{0:T(128)} %stack.61.place_ref.spot_ref, bf16[1024,2304]{1,0:T(8,128)(2,1)} %get-tuple-element.207.qkv_ref, bf16[1024,768]{1,0:T(8,128)(2,1)} %get-tuple-element.197.ctx_ref.o_ref, ...), custom_call_target="tpu_custom_call" | custom-call | flops 1150000 | tf_op jit(solution)/shard_map/attn_bwd/pallas_call | solution.py:250
  246.4 3.5 fusion
  250.7 1.6 collective-permute-done.21
  255.1 2.3 fusion.23
  258.0 1.4 collective-permute-start.24
  259.4 27.1 %attn_bwd.3 = (bf16[1024,1536]{1,0:T(8,128)(2,1)}, f32[4,8,1024]{2,1,0:T(8,128)}, f32[4,8,384]{2,1,0:T(8,128)}, bf16[384,1536]{1,0:T(8,128)(2,1)}, bf16[384,1536]{1,0:T(8,128)(2,1)}) custom-call(s32[5]{0:T(128)} %stack.61.place_ref.spot_ref, bf16[1024,2304]{1,0:T(8,128)(2,1)} %get-tuple-element.207.qkv_ref, ...), custom_call_target="tpu_custom_call" | custom-call | flops 1150000 | tf_op jit(solution)/shard_map/attn_bwd/pallas_call | solution.py:250
  286.6 1.5 collective-permute-start.27
  288.1 2.7 fusion.1
  293.5 2.0 fusion.9
  301.8 3.3 fusion.63
  306.5 4.3 %add_add_fusion = f32[1024,768]{1,0:T(8,128)} fusion(f32[1024,768]{1,0:T(8,128)S(1)} %copy-done.30, f32[1024,768]{1,0:T(8,128)S(1)} %fusion.63, bf16[1024,1536]{1,0:T(8,128)(2,1)S(1)} %copy-done.31, bf16[768,1536]{1,0:T(8,128)(2,1)S(1)} %copy-done.4), kind=kOutput, calls=%fused_computation | convolution fusion | flops 2417491968 | bytes 14942208 | tf_op jit(solution)/shard_map/dot_general | solution.py:53
  312.2 2.6 fusion.11
  316.2 2.7 collective-permute-start.38
  320.4 2.1 fusion.21
  324.2 7.0 %collective-permute-done.38 = bf16[24,3840]{1,0:T(8,128)(2,1)S(1)} collective-permute-done((bf16[24,3840]{1,0:T(8,128)(2,1)S(1)}, bf16[24,3840]{1,0:T(8,128)(2,1)S(1)}, u32[]{:S(2)}, u32[]{:S(2)}) %collective-permute-start.38) | collective-permute-done | bytes 184352 | tf_op jit(solution)/shard_map/ppermute | solution.py:676
  331.2 2.8 collective-permute-done.39
  339.9 9.9 %collective-permute-done.35 = bf16[40,2304]{1,0:T(8,128)(2,1)S(1)} collective-permute-done((bf16[40,2304]{1,0:T(8,128)(2,1)S(1)}, bf16[40,2304]{1,0:T(8,128)(2,1)S(1)}, u32[]{:S(2)}, u32[]{:S(2)}) %collective-permute-start.35) | collective-permute-done | bytes 184352 | tf_op jit(solution)/shard_map/ppermute | solution.py:676
  349.8 2.9 collective-permute-done.36
  (229 shorter events, 65.5 us)
Async XLA Ops:
  7.2 44.1 %copy-start.29 = (s32[1023]{0:T(1024)S(1)}, s32[1023]{0:T(1024)}, u32[]{:S(2)}) copy-start(s32[1023]{0:T(1024)} %param.26) | copy-start | bytes 12280
  7.2 102.5 %all-gather.3.cloned.1.call-start = ((), (), s32[]{:S(2)}) async-start(), calls=%async_computation | async-start | bytes 4866048 | tf_op jit(solution)/shard_map/all_gather | solution.py:1015
  9.0 142.0 %all-gather.5.cloned.1.call-start = ((), (), s32[]{:S(2)}) async-start(), calls=%async_computation.1 | async-start | bytes 4866048 | tf_op jit(solution)/shard_map/all_gather | solution.py:1049
  11.3 43.4 %copy-start.10 = (s32[5]{0:T(128)S(1)}, s32[5]{0:T(128)}, u32[]{:S(2)}) copy-start(s32[5]{0:T(128)} %stack.61.place_ref.spot_ref) | copy-start | bytes 64
  16.0 8.6 %collective-permute-start = (bf16[1,64,768]{2,1,0:T(8,128)(2,1)}, bf16[1,64,768]{2,1,0:T(8,128)(2,1)S(1)}, u32[]{:S(2)}, u32[]{:S(2)}) collective-permute-start(bf16[1,64,768]{2,1,0:T(8,128)(2,1)} %bitcast.291), channel_id=1, source_target_pairs={{0,8},{4,12},{8,16},{12,20},{16,24},{20,28},{24,0},{28,4},{1,9},{5... | collective-permute-start | bytes 294920 | tf_op jit(solution)/shard_map/ppermute | solution.py:676
  17.3 8.9 %collective-permute-start.1 = (bf16[1,64,768]{2,1,0:T(8,128)(2,1)}, bf16[1,64,768]{2,1,0:T(8,128)(2,1)S(1)}, u32[]{:S(2)}, u32[]{:S(2)}) collective-permute-start(bf16[1,64,768]{2,1,0:T(8,128)(2,1)} %bitcast.292), channel_id=1, source_target_pairs={{0,16},{4,20},{8,24},{12,28},{16,0},{20,4},{24,8},{28,12},{1,17},{... | collective-permute-start | bytes 294920 | tf_op jit(solution)/shard_map/ppermute | solution.py:676
  18.3 11.6 %collective-permute-start.2 = (bf16[1,64,768]{2,1,0:T(8,128)(2,1)}, bf16[1,64,768]{2,1,0:T(8,128)(2,1)S(1)}, u32[]{:S(2)}, u32[]{:S(2)}) collective-permute-start(bf16[1,64,768]{2,1,0:T(8,128)(2,1)} %bitcast.293), channel_id=1, source_target_pairs={{0,24},{4,28},{8,0},{12,4},{16,8},{20,12},{24,16},{28,20},{1,25},{... | collective-permute-start | bytes 294920 | tf_op jit(solution)/shard_map/ppermute | solution.py:676
  33.4 17.3 %collective-permute-start.3 = (bf16[4,64,768]{2,1,0:T(8,128)(2,1)}, bf16[4,64,768]{2,1,0:T(8,128)(2,1)S(1)}, u32[]{:S(2)}, u32[]{:S(2)}) collective-permute-start(bf16[4,64,768]{2,1,0:T(8,128)(2,1)} %join.4.refs_0_), channel_id=1, source_target_pairs={{0,4},{4,0},{8,12},{12,8},{16,20},{20,16},{24,28},{28,24},{1,5},{5... | collective-permute-start | bytes 1179656 | tf_op jit(solution)/shard_map/ppermute | solution.py:676
  34.6 4.9 %collective-permute-start.4 = (bf16[1,144,384]{2,1,0:T(8,128)(2,1)}, bf16[1,144,384]{2,1,0:T(8,128)(2,1)S(1)}, u32[]{:S(2)}, u32[]{:S(2)}) collective-permute-start(bf16[1,144,384]{2,1,0:T(8,128)(2,1)} %bitcast.287), channel_id=1, source_target_pairs={{0,8},{4,12},{8,16},{12,20},{16,24},{20,28},{24,0},{28,4},{1,9},{5... | collective-permute-start | bytes 331784 | tf_op jit(solution)/shard_map/ppermute | solution.py:676
  34.6 5.7 %collective-permute-start.5 = (bf16[1,144,384]{2,1,0:T(8,128)(2,1)}, bf16[1,144,384]{2,1,0:T(8,128)(2,1)S(1)}, u32[]{:S(2)}, u32[]{:S(2)}) collective-permute-start(bf16[1,144,384]{2,1,0:T(8,128)(2,1)} %bitcast.288), channel_id=1, source_target_pairs={{0,16},{4,20},{8,24},{12,28},{16,0},{20,4},{24,8},{28,12},{1,17},{... | collective-permute-start | bytes 331784 | tf_op jit(solution)/shard_map/ppermute | solution.py:676
  35.0 15.7 %collective-permute-start.6 = (bf16[1,144,384]{2,1,0:T(8,128)(2,1)}, bf16[1,144,384]{2,1,0:T(8,128)(2,1)S(1)}, u32[]{:S(2)}, u32[]{:S(2)}) collective-permute-start(bf16[1,144,384]{2,1,0:T(8,128)(2,1)} %bitcast.289), channel_id=1, source_target_pairs={{0,24},{4,28},{8,0},{12,4},{16,8},{20,12},{24,16},{28,20},{1,25},{... | collective-permute-start | bytes 331784 | tf_op jit(solution)/shard_map/ppermute | solution.py:676
  36.1 18.6 %collective-permute-start.7 = (bf16[4,64,768]{2,1,0:T(8,128)(2,1)}, bf16[4,64,768]{2,1,0:T(8,128)(2,1)S(1)}, u32[]{:S(2)}, u32[]{:S(2)}) collective-permute-start(bf16[4,64,768]{2,1,0:T(8,128)(2,1)} %join.4.refs_0_), channel_id=1, source_target_pairs={{0,1},{1,0},{2,3},{3,2},{4,5},{5,4},{6,7},{7,6},{8,9},{9,8},{10,11... | collective-permute-start | bytes 1179656 | tf_op jit(solution)/shard_map/ppermute | solution.py:676
  50.7 4.0 %collective-permute-start.8 = (bf16[4,64,768]{2,1,0:T(8,128)(2,1)S(1)}, bf16[4,64,768]{2,1,0:T(8,128)(2,1)S(1)}, u32[]{:S(2)}, u32[]{:S(2)}) collective-permute-start(bf16[4,64,768]{2,1,0:T(8,128)(2,1)S(1)} %collective-permute-done.3.refs_1_), channel_id=1, source_target_pairs={{0,1},{1,0},{2,3},{3,2},{4,5},{5,4},{6,7},{7,6},{8,9},{9,8},{10,11... | collective-permute-start | bytes 1179656 | tf_op jit(solution)/shard_map/ppermute | solution.py:676
  51.6 12.1 %copy-start.11 = (pred[1023,256]{1,0:T(8,128)(4,1)}, pred[1023,256]{1,0:T(8,128)(4,1)S(1)}, u32[]{:S(2)}) copy-start(pred[1023,256]{1,0:T(8,128)(4,1)S(1)} %iota_compare_fusion) | copy-start | bytes 785668
  53.5 10.2 %collective-permute-start.10 = (bf16[4,96,384]{2,1,0:T(8,128)(2,1)}, bf16[4,96,384]{2,1,0:T(8,128)(2,1)}, u32[]{:S(2)}, u32[]{:S(2)}) collective-permute-start(bf16[4,96,384]{2,1,0:T(8,128)(2,1)} %get-tuple-element.174.refs_0_), channel_id=1, source_target_pairs={{0,2},{1,3},{2,0},{3,1},{4,6},{5,7},{6,4},{7,5},{8,10},{9,11},{10,... | collective-permute-start | bytes 884744 | tf_op jit(solution)/shard_map/ppermute | solution.py:676
  54.7 9.0 %collective-permute-start.9 = (bf16[4,48,384]{2,1,0:T(8,128)(2,1)}, bf16[4,48,384]{2,1,0:T(8,128)(2,1)S(1)}, u32[]{:S(2)}, u32[]{:S(2)}) collective-permute-start(bf16[4,48,384]{2,1,0:T(8,128)(2,1)} %get-tuple-element.168.refs_0_), channel_id=1, source_target_pairs={{0,4},{4,0},{8,12},{12,8},{16,20},{20,16},{24,28},{28,24},{1,5},{5... | collective-permute-start | bytes 442376 | tf_op jit(solution)/shard_map/ppermute | solution.py:676
  65.7 21.1 %copy-start.5 = (bf16[8,96,384]{2,1,0:T(8,128)(2,1)S(1)}, bf16[8,96,384]{2,1,0:T(8,128)(2,1)}, u32[]{:S(2)}) copy-start(bf16[8,96,384]{2,1,0:T(8,128)(2,1)} %join.7.refs_4_) | copy-start | bytes 1769476
  65.7 17.8 %collective-permute-start.12 = (bf16[8,96,384]{2,1,0:T(8,128)(2,1)}, bf16[8,96,384]{2,1,0:T(8,128)(2,1)S(1)}, u32[]{:S(2)}, u32[]{:S(2)}) collective-permute-start(bf16[8,96,384]{2,1,0:T(8,128)(2,1)} %join.7.refs_4_), channel_id=1, source_target_pairs={{0,4},{4,0},{8,12},{12,8},{16,20},{20,16},{24,28},{28,24},{1,5},{5... | collective-permute-start | bytes 1769480 | tf_op jit(solution)/shard_map/ppermute | solution.py:676
  68.8 15.4 %copy-start.9 = (bf16[8,48,384]{2,1,0:T(8,128)(2,1)S(1)}, bf16[8,48,384]{2,1,0:T(8,128)(2,1)}, u32[]{:S(2)}) copy-start(bf16[8,48,384]{2,1,0:T(8,128)(2,1)} %join.6.refs_0_) | copy-start | bytes 884740
  68.8 11.5 %collective-permute-start.11 = (bf16[8,48,384]{2,1,0:T(8,128)(2,1)}, bf16[8,48,384]{2,1,0:T(8,128)(2,1)S(1)}, u32[]{:S(2)}, u32[]{:S(2)}) collective-permute-start(bf16[8,48,384]{2,1,0:T(8,128)(2,1)} %join.6.refs_0_), channel_id=1, source_target_pairs={{0,2},{1,3},{2,0},{3,1},{4,6},{5,7},{6,4},{7,5},{8,10},{9,11},{10,... | collective-permute-start | bytes 884744 | tf_op jit(solution)/shard_map/ppermute | solution.py:676
  69.1 17.2 %collective-permute-start.15 = (bf16[8,96,384]{2,1,0:T(8,128)(2,1)}, bf16[8,96,384]{2,1,0:T(8,128)(2,1)}, u32[]{:S(2)}, u32[]{:S(2)}) collective-permute-start(bf16[8,96,384]{2,1,0:T(8,128)(2,1)} %join.7.refs_4_), channel_id=1, source_target_pairs={{0,1},{1,0},{2,3},{3,2},{4,5},{5,4},{6,7},{7,6},{8,9},{9,8},{10,11... | collective-permute-start | bytes 1769480 | tf_op jit(solution)/shard_map/ppermute | solution.py:676
  83.5 3.3 collective-permute-start.16
  84.3 2.0 collective-permute-start.13
  84.3 2.5 collective-permute-start.14
  185.8 11.9 %collective-permute-start.17 = (bf16[4,4,96,768]{3,2,1,0:T(8,128)(2,1)}, bf16[4,4,96,768]{3,2,1,0:T(8,128)(2,1)}, u32[]{:S(2)}, u32[]{:S(2)}) collective-permute-start(bf16[4,4,96,768]{3,2,1,0:T(8,128)(2,1)} %get-tuple-element.217), channel_id=1, source_target_pairs={{0,1},{1,0},{2,3},{3,2},{4,5},{5,4},{6,7},{7,6},{8,9},{9,8},{10,11... | collective-permute-start | bytes 7077896 | tf_op jit(solution)/shard_map/ppermute | solution.py:676
  199.7 27.4 %collective-permute-start.18 = (bf16[2,4,96,768]{3,2,1,0:T(8,128)(2,1)S(1)}, bf16[2,4,96,768]{3,2,1,0:T(8,128)(2,1)}, u32[]{:S(2)}, u32[]{:S(2)}) collective-permute-start(bf16[2,4,96,768]{3,2,1,0:T(8,128)(2,1)S(1)} %fusion.2), channel_id=1, source_target_pairs={{0,2},{1,3},{2,0},{3,1},{4,6},{5,7},{6,4},{7,5},{8,10},{9,11},{10,... | collective-permute-start | bytes 3538952 | tf_op jit(solution)/shard_map/ppermute | solution.py:676
  227.1 19.3 %collective-permute-start.20 = (bf16[384,3840]{1,0:T(8,128)(2,1)}, bf16[384,3840]{1,0:T(8,128)(2,1)}, u32[]{:S(2)}, u32[]{:S(2)}) collective-permute-start(bf16[384,3840]{1,0:T(8,128)(2,1)} %get-tuple-element.237), channel_id=1, source_target_pairs={{0,1},{1,0},{2,3},{3,2},{4,5},{5,4},{6,7},{7,6},{8,9},{9,8},{10,11... | collective-permute-start | bytes 8847368 | tf_op jit(solution)/shard_map/ppermute | solution.py:676
  229.9 16.5 %collective-permute-start.19 = (bf16[4,96,768]{2,1,0:T(8,128)(2,1)S(1)}, bf16[4,96,768]{2,1,0:T(8,128)(2,1)S(1)}, u32[]{:S(2)}, u32[]{:S(2)}) collective-permute-start(bf16[4,96,768]{2,1,0:T(8,128)(2,1)S(1)} %fusion.3), channel_id=1, source_target_pairs={{0,4},{4,0},{8,12},{12,8},{16,20},{20,16},{24,28},{28,24},{1,5},{5... | collective-permute-start | bytes 1769480 | tf_op jit(solution)/shard_map/ppermute | solution.py:676
  249.9 36.7 %collective-permute-start.26 = (bf16[2,4,24,3840]{3,2,1,0:T(8,128)(2,1)}, bf16[2,4,24,3840]{3,2,1,0:T(8,128)(2,1)}, u32[]{:S(2)}, u32[]{:S(2)}) collective-permute-start(bf16[2,4,24,3840]{3,2,1,0:T(8,128)(2,1)} %fusion), channel_id=1, source_target_pairs={{0,4},{4,0},{8,12},{12,8},{16,20},{20,16},{24,28},{28,24},{1,5},{5... | collective-permute-start | bytes 4423688 | tf_op jit(solution)/shard_map/ppermute | solution.py:676
  250.2 2.2 collective-permute-start.21
  254.0 32.6 %collective-permute-start.22 = (bf16[2,4,24,768]{3,2,1,0:T(8,128)(2,1)}, bf16[2,4,24,768]{3,2,1,0:T(8,128)(2,1)}, u32[]{:S(2)}, u32[]{:S(2)}) collective-permute-start(bf16[2,4,24,768]{3,2,1,0:T(8,128)(2,1)} %fusion.18), channel_id=1, source_target_pairs={{0,2},{1,3},{2,0},{3,1},{4,6},{5,7},{6,4},{7,5},{8,10},{9,11},{10,... | collective-permute-start | bytes 884744 | tf_op jit(solution)/shard_map/ppermute | solution.py:676
  257.4 29.1 %collective-permute-start.23 = (bf16[96,768]{1,0:T(8,128)(2,1)}, bf16[96,768]{1,0:T(8,128)(2,1)}, u32[]{:S(2)}, u32[]{:S(2)}) collective-permute-start(bf16[96,768]{1,0:T(8,128)(2,1)} %get-tuple-element.366), channel_id=1, source_target_pairs={{0,8},{4,12},{8,16},{12,20},{16,24},{20,28},{24,0},{28,4},{1,9},{5... | collective-permute-start | bytes 442376 | tf_op jit(solution)/shard_map/ppermute | solution.py:676
  258.0 28.6 %collective-permute-start.24 = (bf16[96,768]{1,0:T(8,128)(2,1)}, bf16[96,768]{1,0:T(8,128)(2,1)}, u32[]{:S(2)}, u32[]{:S(2)}) collective-permute-start(bf16[96,768]{1,0:T(8,128)(2,1)} %get-tuple-element.365), channel_id=1, source_target_pairs={{0,16},{4,20},{8,24},{12,28},{16,0},{20,4},{24,8},{28,12},{1,17},{... | collective-permute-start | bytes 442376 | tf_op jit(solution)/shard_map/ppermute | solution.py:676
  259.4 27.2 %collective-permute-start.25 = (bf16[96,768]{1,0:T(8,128)(2,1)S(1)}, bf16[96,768]{1,0:T(8,128)(2,1)}, u32[]{:S(2)}, u32[]{:S(2)}) collective-permute-start(bf16[96,768]{1,0:T(8,128)(2,1)S(1)} %get-tuple-element.364), channel_id=1, source_target_pairs={{0,24},{4,28},{8,0},{12,4},{16,8},{20,12},{24,16},{28,20},{1,25},{... | collective-permute-start | bytes 442376 | tf_op jit(solution)/shard_map/ppermute | solution.py:676
  286.6 7.0 %collective-permute-start.27 = (bf16[384,1536]{1,0:T(8,128)(2,1)}, bf16[384,1536]{1,0:T(8,128)(2,1)}, u32[]{:S(2)}, u32[]{:S(2)}) collective-permute-start(bf16[384,1536]{1,0:T(8,128)(2,1)} %get-tuple-element.269), channel_id=1, source_target_pairs={{0,1},{1,0},{2,3},{3,2},{4,5},{5,4},{6,7},{7,6},{8,9},{9,8},{10,11... | collective-permute-start | bytes 3538952 | tf_op jit(solution)/shard_map/ppermute | solution.py:676
  290.8 19.9 %collective-permute-start.31 = (bf16[4,24,3840]{2,1,0:T(8,128)(2,1)}, bf16[4,24,3840]{2,1,0:T(8,128)(2,1)}, u32[]{:S(2)}, u32[]{:S(2)}) collective-permute-start(bf16[4,24,3840]{2,1,0:T(8,128)(2,1)} %fusion.1), channel_id=1, source_target_pairs={{0,2},{1,3},{2,0},{3,1},{4,6},{5,7},{6,4},{7,5},{8,10},{9,11},{10,... | collective-permute-start | bytes 2211848 | tf_op jit(solution)/shard_map/ppermute | solution.py:676
  292.3 18.5 %collective-permute-start.30 = (bf16[4,24,768]{2,1,0:T(8,128)(2,1)S(1)}, bf16[4,24,768]{2,1,0:T(8,128)(2,1)}, u32[]{:S(2)}, u32[]{:S(2)}) collective-permute-start(bf16[4,24,768]{2,1,0:T(8,128)(2,1)S(1)} %fusion.22), channel_id=1, source_target_pairs={{0,4},{4,0},{8,12},{12,8},{16,20},{20,16},{24,28},{28,24},{1,5},{5... | collective-permute-start | bytes 442376 | tf_op jit(solution)/shard_map/ppermute | solution.py:676
  296.6 22.4 %collective-permute-start.32 = (bf16[2,4,24,1536]{3,2,1,0:T(8,128)(2,1)}, bf16[2,4,24,1536]{3,2,1,0:T(8,128)(2,1)}, u32[]{:S(2)}, u32[]{:S(2)}) collective-permute-start(bf16[2,4,24,1536]{3,2,1,0:T(8,128)(2,1)} %fusion.9), channel_id=1, source_target_pairs={{0,4},{4,0},{8,12},{12,8},{16,20},{20,16},{24,28},{28,24},{1,5},{5... | collective-permute-start | bytes 1769480 | tf_op jit(solution)/shard_map/ppermute | solution.py:676
  300.8 4.4 %collective-permute-start.28 = (bf16[16,1536]{1,0:T(8,128)(2,1)S(1)}, bf16[16,1536]{1,0:T(8,128)(2,1)S(1)}, u32[]{:S(2)}, u32[]{:S(2)}) collective-permute-start(bf16[16,1536]{1,0:T(8,128)(2,1)S(1)} %fusion.35), channel_id=1, source_target_pairs={{0,1},{1,0},{2,3},{3,2},{4,5},{5,4},{6,7},{7,6},{8,9},{9,8},{10,11... | collective-permute-start | bytes 147464 | tf_op jit(solution)/shard_map/ppermute | solution.py:676
  305.2 7.0 %collective-permute-start.29 = (bf16[16,1536]{1,0:T(8,128)(2,1)S(1)}, bf16[16,1536]{1,0:T(8,128)(2,1)S(1)}, u32[]{:S(2)}, u32[]{:S(2)}) collective-permute-start(bf16[16,1536]{1,0:T(8,128)(2,1)S(1)} %fusion.60), channel_id=1, source_target_pairs={{0,4},{4,0},{8,12},{12,8},{16,20},{20,16},{24,28},{28,24},{1,5},{5... | collective-permute-start | bytes 147464 | tf_op jit(solution)/shard_map/ppermute | solution.py:676
  314.7 9.4 %collective-permute-start.37 = (bf16[24,3840]{1,0:T(8,128)(2,1)}, bf16[24,3840]{1,0:T(8,128)(2,1)S(1)}, u32[]{:S(2)}, u32[]{:S(2)}) collective-permute-start(bf16[24,3840]{1,0:T(8,128)(2,1)} %get-tuple-element.363), channel_id=1, source_target_pairs={{0,8},{4,12},{8,16},{12,20},{16,24},{20,28},{24,0},{28,4},{1,9},{5... | collective-permute-start | bytes 552968 | tf_op jit(solution)/shard_map/ppermute | solution.py:676
  316.2 15.0 %collective-permute-start.38 = (bf16[24,3840]{1,0:T(8,128)(2,1)S(1)}, bf16[24,3840]{1,0:T(8,128)(2,1)S(1)}, u32[]{:S(2)}, u32[]{:S(2)}) collective-permute-start(bf16[24,3840]{1,0:T(8,128)(2,1)S(1)} %get-tuple-element.362), channel_id=1, source_target_pairs={{0,16},{4,20},{8,24},{12,28},{16,0},{20,4},{24,8},{28,12},{1,17},{... | collective-permute-start | bytes 552968 | tf_op jit(solution)/shard_map/ppermute | solution.py:676
  318.9 15.1 %collective-permute-start.39 = (bf16[24,3840]{1,0:T(8,128)(2,1)S(1)}, bf16[24,3840]{1,0:T(8,128)(2,1)S(1)}, u32[]{:S(2)}, u32[]{:S(2)}) collective-permute-start(bf16[24,3840]{1,0:T(8,128)(2,1)S(1)} %get-tuple-element.361), channel_id=1, source_target_pairs={{0,24},{4,28},{8,0},{12,4},{16,8},{20,12},{24,16},{28,20},{1,25},{... | collective-permute-start | bytes 552968 | tf_op jit(solution)/shard_map/ppermute | solution.py:676
  320.0 13.9 %collective-permute-start.33 = (bf16[112,1536]{1,0:T(8,128)(2,1)S(1)}, bf16[112,1536]{1,0:T(8,128)(2,1)S(1)}, u32[]{:S(2)}, u32[]{:S(2)}) collective-permute-start(bf16[112,1536]{1,0:T(8,128)(2,1)S(1)} %pad_maximum_fusion), channel_id=1, source_target_pairs={{0,2},{1,3},{2,0},{3,1},{4,6},{5,7},{6,4},{7,5},{8,10},{9,11},{10,... | collective-permute-start | bytes 1032200 | tf_op jit(solution)/shard_map/ppermute | solution.py:676
  335.3 4.7 %collective-permute-start.34 = (bf16[40,2304]{1,0:T(8,128)(2,1)S(1)}, bf16[40,2304]{1,0:T(8,128)(2,1)S(1)}, u32[]{:S(2)}, u32[]{:S(2)}) collective-permute-start(bf16[40,2304]{1,0:T(8,128)(2,1)S(1)} %get-tuple-element.378), channel_id=1, source_target_pairs={{0,8},{4,12},{8,16},{12,20},{16,24},{20,28},{24,0},{28,4},{1,9},{5... | collective-permute-start | bytes 552968 | tf_op jit(solution)/shard_map/ppermute | solution.py:676
  335.3 14.5 %collective-permute-start.35 = (bf16[40,2304]{1,0:T(8,128)(2,1)S(1)}, bf16[40,2304]{1,0:T(8,128)(2,1)S(1)}, u32[]{:S(2)}, u32[]{:S(2)}) collective-permute-start(bf16[40,2304]{1,0:T(8,128)(2,1)S(1)} %get-tuple-element.379), channel_id=1, source_target_pairs={{0,16},{4,20},{8,24},{12,28},{16,0},{20,4},{24,8},{28,12},{1,17},{... | collective-permute-start | bytes 552968 | tf_op jit(solution)/shard_map/ppermute | solution.py:676
  335.8 17.0 %collective-permute-start.36 = (bf16[40,2304]{1,0:T(8,128)(2,1)S(1)}, bf16[40,2304]{1,0:T(8,128)(2,1)S(1)}, u32[]{:S(2)}, u32[]{:S(2)}) collective-permute-start(bf16[40,2304]{1,0:T(8,128)(2,1)S(1)} %get-tuple-element.377), channel_id=1, source_target_pairs={{0,24},{4,28},{8,0},{12,4},{16,8},{20,12},{24,16},{28,20},{1,25},{... | collective-permute-start | bytes 552968 | tf_op jit(solution)/shard_map/ppermute | solution.py:676
  337.1 22.2 %copy-start.1 = (bf16[96,3072]{1,0:T(8,128)(2,1)S(1)}, bf16[96,3072]{1,0:T(8,128)(2,1)}, u32[]{:S(2)}) copy-start(bf16[96,3072]{1,0:T(8,128)(2,1)} %param.31) | copy-start | bytes 1769476
  (28 other events, 152.1 us)
Sparse Core Ops, SparseCore 0:
  11.0 73.2 all-gather.2
  87.1 63.8 all-gather.4

commit v2 on v1

--- a/solution.py
+++ b/solution.py
@@ -448,7 +448,7 @@
             sum_ref[1:2, :] += jnp.sum(grad_out, axis=0, keepdims=True)
             sum_ref[2:3, :] += jnp.sum(grad_low.astype(F32), axis=0, keepdims=True)
 
-        row_chunks(rows, 128, step)
+        row_chunks(rows, 256, step)
         total = jnp.zeros((1, width), F32)
         for first, value in firsts.items():
             total = total + value * hid_ref[first : first + 8, :].astype(F32)[0:1, :]
@@ -508,7 +508,7 @@
 def act_bwd_kernel(dr_ref, slope_ref, w2_ref, din_ref, db_ref):
     grad = dr_ref[...]
     wide = w2_ref.shape[0]
-    size = min(256, wide)
+    size = min(512, wide)
     for start in range(0, wide, size):
         cols = slice(start, start + size)
         d_act = contract(grad, w2_ref[cols, :], 1, 1)
@@ -520,7 +520,7 @@
 def act_bwd(grad, slope, w_outer):
     rows, hidden = slope.shape
     width = grad.shape[1]
-    size = min(512, hidden)
+    size = min(1024, hidden)
     cols = pl.BlockSpec((rows, size), lambda n: (0, n))
     return pl.pallas_call(
         act_bwd_kernel,
@@ -593,7 +593,7 @@
             sum_ref[1:2, :] += jnp.sum(grad_out, axis=0, keepdims=True)
             sum_ref[2:3, :] += jnp.sum(grad_low.astype(F32), axis=0, keepdims=True)
 
-        row_chunks(rows, 128, step)
+        row_chunks(rows, 256, step)
         tile[...] = contract(ctx_buf[...], grad_ref[...], 0, 0)
 
     split_rows(place_ref[3], tile, *blocks, kept, sent)

time: 368 us -> 367 us (level)
  no operation moved by 1% of the time
where the time goes in v2:
time: 367 us; the launch traced here: 365 us
  Pallas kernels  176 us (48%)
  waiting for transfers between devices  63.5 us (17%)
  starting transfers between devices  36.1 us (10%)
  local copies, waits for them, and re-layouts  30.8 us (8%)
  other arithmetic  30.5 us (8%)
  between operations  14.8 us (4%)
  matrix products  8.39 us (2%)
  blocking collectives  5.29 us (1%)
    ppermute x40, waiting for transfers between devices, move(): lax.ppermute(value, axis, shifted(self.lengths[axis], self.sizes[dim], st...  51.7 us
    pallas_call x2, Pallas kernels, attn_bwd(): pl.pallas_call(partial(attn_bwd_kernel, blocks), grid_spec=pltpu.Prefetch...  42.3 us
    ppermute x40, starting transfers between devices, move(): lax.ppermute(value, axis, shifted(self.lengths[axis], self.sizes[dim], st...  36 us
    pallas_call x1, Pallas kernels, ffn_in(): pl.pallas_call(ffn_in_kernel, grid=(hidden // size,), in_specs=[whole, wh...  29.5 us
    pallas_call x2, Pallas kernels, attn_fwd(): pl.pallas_call(attn_fwd_kernel, grid=(pairs, micros), in_specs=[pl.BlockS...  27.1 us
    pallas_call x1, Pallas kernels, inner_bwd(): pl.pallas_call(partial(inner_bwd_kernel, blocks), grid_spec=pltpu.Prefetc...  21.7 us
    convert_element_type x12, other arithmetic, step(): sent.append(total.astype(BF))  20.8 us
    pallas_call x1, Pallas kernels, outer_bwd(): pl.pallas_call(partial(outer_bwd_kernel, blocks), grid_spec=pltpu.Prefetc...  16.6 us
  transfers between devices with their start and end apart: 42, of which 15 were waited for; matrix products, arithmetic and copies ran while one was open for 13% of the time, Pallas kernels for 41%

profile of v2, /device:TPU:9, one launch (start us, length us, event | category | flops | bytes accessed | tf_op | source)
XLA Modules:
  0.0 365.4 jit_solution(1020873471245201376)
XLA Ops:
  11.3 1.5 stack.71
  13.5 2.5 pack.1
  18.3 1.5 collective-permute-start.2
  24.6 1.6 collective-permute-done.1.refs_2_
  26.2 3.7 %collective-permute-done.2.refs_3_ = bf16[1,64,768]{2,1,0:T(8,128)(2,1)S(1)} collective-permute-done((bf16[1,64,768]{2,1,0:T(8,128)(2,1)}, bf16[1,64,768]{2,1,0:T(8,128)(2,1)S(1)}, u32[]{:S(2)}, u32[]{:S(2)}) %collective-permute-start.2) | collective-permute-done | bytes 98336 | tf_op jit(solution)/shard_map/ppermute | solution.py:676
  29.9 1.6 constant_dynamic-slice_fusion.1
  31.6 1.8 join.4.refs_0_
  36.1 3.4 collective-permute-start.7
  40.4 10.4 %collective-permute-done.6.refs_3_ = bf16[1,144,384]{2,1,0:T(8,128)(2,1)S(1)} collective-permute-done((bf16[1,144,384]{2,1,0:T(8,128)(2,1)}, bf16[1,144,384]{2,1,0:T(8,128)(2,1)S(1)}, u32[]{:S(2)}, u32[]{:S(2)}) %collective-permute-start.6) | collective-permute-done | bytes 110624 | tf_op jit(solution)/shard_map/ppermute | solution.py:676
  51.6 1.9 join.5
  55.7 3.3 place_blocks.2
  63.7 2.0 join.7.refs_4_
  65.7 1.5 collective-permute-start.12
  67.1 1.7 join.6.refs_0_
  70.5 9.8 %attn_fwd.2 = (bf16[1024,2304]{1,0:T(8,128)(2,1)}, bf16[1024,768]{1,0:T(8,128)(2,1)}, bf16[2,12,512,512]{3,2,1,0:T(8,128)(2,1)}) custom-call(bf16[1024,768]{1,0:T(8,128)(2,1)} %bitcast.252, bf16[768,768]{1,0:T(8,128)(2,1)} %copy-done.7, f32[1,2304]{1,0:T(1,128)} %reshape.639.b_ref, f32[6,8,1024]{2,1,0:T(8,128)} %pad.46.dist_ref, f32[2,8,512]{2,1,0:T(8,128)} %pad.43.mask_ref), custom_call_target="tpu_custom_call" | custom-call | flops 1150000 | tf_op jit(solution)/shard_map/attn_fwd/pallas_call | solution.py:155
  80.4 3.1 collective-permute-done.12.refs_5_
  84.8 1.5 collective-permute-done.13.refs_2_
  86.7 3.3 place_blocks.3
  91.0 1.4 copy-done.3
  92.4 17.3 %attn_fwd.3 = (bf16[1024,2304]{1,0:T(8,128)(2,1)}, bf16[1024,768]{1,0:T(8,128)(2,1)}, bf16[2,12,512,512]{3,2,1,0:T(8,128)(2,1)}) custom-call(bf16[1024,768]{1,0:T(8,128)(2,1)} %bitcast.253, bf16[768,1536]{1,0:T(8,128)(2,1)} %copy-done.3, f32[1,2304]{1,0:T(1,128)} %reshape.639.b_ref, ...), custom_call_target="tpu_custom_call", output_to_operand_aliasing={{0}: (5, {}), {1}: (6, {}), {2}: (7, {})} | custom-call | flops 1150000 | tf_op jit(solution)/shard_map/attn_fwd/pallas_call | solution.py:155
  109.7 29.5 %ffn_in.1 = (f32[1024,768]{1,0:T(8,128)}, f32[1024,1]{1,0:T(8,128)}, bf16[1024,768]{1,0:T(8,128)(2,1)}, bf16[1024,3072]{1,0:T(8,128)(2,1)}, bf16[1024,3072]{1,0:T(8,128)(2,1)}) custom-call(bf16[1024,768]{1,0:T(8,128)(2,1)} %bitcast.254, bf16[1024,768]{1,0:T(8,128)(2,1)} %get-tuple-element.197.ctx_ref.o_ref, bf16[768,768]{1,0:T(8,128)(2,1)} %copy-done.2, ...), custom_call_target="tpu_custom_call" | custom-call | flops 1150000 | tf_op jit(solution)/shard_map/ffn_in/pallas_call | solution.py:331
  139.2 11.8 %all-gather.5.cloned.1.call-done.w_ref.w2_ref = bf16[3072,768]{1,0:T(8,128)(2,1)} async-done(((bf16[96,768]{1,0:T(8,128)(2,1)}), bf16[3072,768]{1,0:T(8,128)(2,1)}) %all-gather.5.cloned.1.call-update) | async-done | bytes 4718608 | tf_op jit(solution)/shard_map/all_gather | solution.py:1049
  151.0 11.2 %ffn_out.1 = (f32[1024,768]{1,0:T(8,128)}, f32[1024,1]{1,0:T(8,128)}, bf16[1024,768]{1,0:T(8,128)(2,1)}, f32[4,8,128]{2,1,0:T(8,128)}) custom-call(bf16[1024,3072]{1,0:T(8,128)(2,1)} %get-tuple-element.203.act_ref, bf16[3072,768]{1,0:T(8,128)(2,1)} %all-gather.5.cloned.1.call-done.w_ref.w2_ref, f32[1024,768]{1,0:T(8,128)} %get-tuple-element.205.n1_ref, ...), custom_call_target="tpu_custom_call" | custom-call | flops 1150000 | tf_op jit(solution)/shard_map/ffn_out/pallas_call | solution.py:373
  163.1 5.3 %all_gather.11 = f32[2,4,2]{2,0,1:T(2,128)S(1)} all-gather(f32[2,1,2]{2,0,1:T(2,128)S(1)} %reshape_squeeze.20), channel_id=1, replica_groups=mesh['query'=8,'cand'=4] {'cand'}, dimensions={1}, use_global_device_ids=true | all-gather | bytes 80 | tf_op jit(solution)/shard_map/all_gather | solution.py:1098
  169.1 16.6 %outer_bwd.1 = (f32[1024,768]{1,0:T(8,128)}, bf16[1024,768]{1,0:T(8,128)(2,1)}, f32[8,768]{1,0:T(8,128)}, f32[2,128]{1,0:T(2,128)}, bf16[4,4,96,768]{3,2,1,0:T(8,128)(2,1)}, /*index=5*/bf16[4,4,96,768]{3,2,1,0:T(8,128)(2,1)}) custom-call(s32[5]{0:T(128)} %stack.61.place_ref.spot_ref, f32[2,8]{1,0:T(2,128)} %reshape.641.score_ref, s32[2,8]{1,0:T(2,128)} %reshape.636.len_ref, ...), custom_call_target="tpu_custom_call" | custom-call | flops 1150000 | tf_op jit(solution)/shard_map/outer_bwd/pallas_call | solution.py:475
  185.8 11.2 %act_bwd.1 = (bf16[1024,3072]{1,0:T(8,128)(2,1)}, f32[1,3072]{1,0:T(1,128)}) custom-call(bf16[1024,768]{1,0:T(8,128)(2,1)} %get-tuple-element.213.dr_ref, bf16[1024,3072]{1,0:T(8,128)(2,1)} %get-tuple-element.214.slope_ref, bf16[3072,768]{1,0:T(8,128)(2,1)} %all-gather.5.cloned.1.call-done.w_ref.w2_ref), custom_call_target="tpu_custom_call" | custom-call | flops 1150000 | tf_op jit(solution)/shard_map/act_bwd/pallas_call | solution.py:525
  197.0 1.9 fusion.2
  200.1 21.7 %inner_bwd.1 = (f32[1024,768]{1,0:T(8,128)}, bf16[1024,768]{1,0:T(8,128)(2,1)}, f32[8,768]{1,0:T(8,128)}, bf16[384,3840]{1,0:T(8,128)(2,1)}, bf16[384,3840]{1,0:T(8,128)(2,1)}) custom-call(s32[5]{0:T(128)} %stack.61.place_ref.spot_ref, bf16[1024,3072]{1,0:T(8,128)(2,1)} %get-tuple-element.218.din_ref, ...), custom_call_target="tpu_custom_call" | custom-call | flops 1150000 | tf_op jit(solution)/shard_map/inner_bwd/pallas_call | solution.py:614
  221.9 4.5 %collective-permute-done.18 = bf16[2,4,96,768]{3,2,1,0:T(8,128)(2,1)} collective-permute-done((bf16[2,4,96,768]{3,2,1,0:T(8,128)(2,1)S(1)}, bf16[2,4,96,768]{3,2,1,0:T(8,128)(2,1)}, u32[]{:S(2)}, u32[]{:S(2)}) %collective-permute-start.18) | collective-permute-done | bytes 1179680 | tf_op jit(solution)/shard_map/ppermute | solution.py:676
  227.5 1.6 fusion.3
  230.4 15.2 %attn_bwd.2 = (bf16[1024,768]{1,0:T(8,128)(2,1)}, f32[2,8,1024]{2,1,0:T(8,128)}, f32[2,8,384]{2,1,0:T(8,128)}, bf16[384,768]{1,0:T(8,128)(2,1)}, bf16[384,768]{1,0:T(8,128)(2,1)}) custom-call(s32[5]{0:T(128)} %stack.61.place_ref.spot_ref, bf16[1024,2304]{1,0:T(8,128)(2,1)} %get-tuple-element.207.qkv_ref, bf16[1024,768]{1,0:T(8,128)(2,1)} %get-tuple-element.197.ctx_ref.o_ref, ...), custom_call_target="tpu_custom_call" | custom-call | flops 1150000 | tf_op jit(solution)/shard_map/attn_bwd/pallas_call | solution.py:250
  245.6 3.5 fusion
  250.0 1.6 collective-permute-done.21
  254.4 2.3 fusion.23
  257.2 1.4 collective-permute-start.24
  258.7 27.1 %attn_bwd.3 = (bf16[1024,1536]{1,0:T(8,128)(2,1)}, f32[4,8,1024]{2,1,0:T(8,128)}, f32[4,8,384]{2,1,0:T(8,128)}, bf16[384,1536]{1,0:T(8,128)(2,1)}, bf16[384,1536]{1,0:T(8,128)(2,1)}) custom-call(s32[5]{0:T(128)} %stack.61.place_ref.spot_ref, bf16[1024,2304]{1,0:T(8,128)(2,1)} %get-tuple-element.207.qkv_ref, ...), custom_call_target="tpu_custom_call" | custom-call | flops 1150000 | tf_op jit(solution)/shard_map/attn_bwd/pallas_call | solution.py:250
  285.8 1.5 collective-permute-start.27
  287.4 2.7 fusion.1
  292.8 2.0 fusion.9
  301.1 3.3 fusion.63
  305.7 4.3 %add_add_fusion = f32[1024,768]{1,0:T(8,128)} fusion(f32[1024,768]{1,0:T(8,128)S(1)} %copy-done.30, f32[1024,768]{1,0:T(8,128)S(1)} %fusion.63, bf16[1024,1536]{1,0:T(8,128)(2,1)S(1)} %copy-done.31, bf16[768,1536]{1,0:T(8,128)(2,1)S(1)} %copy-done.4), kind=kOutput, calls=%fused_computation | convolution fusion | flops 2417491968 | bytes 14942208 | tf_op jit(solution)/shard_map/dot_general | solution.py:53
  311.4 2.6 fusion.11
  315.4 2.7 collective-permute-start.38
  319.6 2.1 fusion.21
  323.4 7.0 %collective-permute-done.38 = bf16[24,3840]{1,0:T(8,128)(2,1)S(1)} collective-permute-done((bf16[24,3840]{1,0:T(8,128)(2,1)S(1)}, bf16[24,3840]{1,0:T(8,128)(2,1)S(1)}, u32[]{:S(2)}, u32[]{:S(2)}) %collective-permute-start.38) | collective-permute-done | bytes 184352 | tf_op jit(solution)/shard_map/ppermute | solution.py:676
  330.4 2.8 collective-permute-done.39
  339.2 9.8 %collective-permute-done.35 = bf16[40,2304]{1,0:T(8,128)(2,1)S(1)} collective-permute-done((bf16[40,2304]{1,0:T(8,128)(2,1)S(1)}, bf16[40,2304]{1,0:T(8,128)(2,1)S(1)}, u32[]{:S(2)}, u32[]{:S(2)}) %collective-permute-start.35) | collective-permute-done | bytes 184352 | tf_op jit(solution)/shard_map/ppermute | solution.py:676
  349.0 2.9 collective-permute-done.36
  (229 shorter events, 65.5 us)
Async XLA Ops:
  7.2 44.1 %copy-start.29 = (s32[1023]{0:T(1024)S(1)}, s32[1023]{0:T(1024)}, u32[]{:S(2)}) copy-start(s32[1023]{0:T(1024)} %param.26) | copy-start | bytes 12280
  7.2 102.5 %all-gather.3.cloned.1.call-start = ((), (), s32[]{:S(2)}) async-start(), calls=%async_computation | async-start | bytes 4866048 | tf_op jit(solution)/shard_map/all_gather | solution.py:1015
  9.0 142.0 %all-gather.5.cloned.1.call-start = ((), (), s32[]{:S(2)}) async-start(), calls=%async_computation.1 | async-start | bytes 4866048 | tf_op jit(solution)/shard_map/all_gather | solution.py:1049
  11.3 43.4 %copy-start.10 = (s32[5]{0:T(128)S(1)}, s32[5]{0:T(128)}, u32[]{:S(2)}) copy-start(s32[5]{0:T(128)} %stack.61.place_ref.spot_ref) | copy-start | bytes 64
  16.0 8.6 %collective-permute-start = (bf16[1,64,768]{2,1,0:T(8,128)(2,1)}, bf16[1,64,768]{2,1,0:T(8,128)(2,1)S(1)}, u32[]{:S(2)}, u32[]{:S(2)}) collective-permute-start(bf16[1,64,768]{2,1,0:T(8,128)(2,1)} %bitcast.291), channel_id=1, source_target_pairs={{0,8},{4,12},{8,16},{12,20},{16,24},{20,28},{24,0},{28,4},{1,9},{5... | collective-permute-start | bytes 294920 | tf_op jit(solution)/shard_map/ppermute | solution.py:676
  17.3 8.9 %collective-permute-start.1 = (bf16[1,64,768]{2,1,0:T(8,128)(2,1)}, bf16[1,64,768]{2,1,0:T(8,128)(2,1)S(1)}, u32[]{:S(2)}, u32[]{:S(2)}) collective-permute-start(bf16[1,64,768]{2,1,0:T(8,128)(2,1)} %bitcast.292), channel_id=1, source_target_pairs={{0,16},{4,20},{8,24},{12,28},{16,0},{20,4},{24,8},{28,12},{1,17},{... | collective-permute-start | bytes 294920 | tf_op jit(solution)/shard_map/ppermute | solution.py:676
  18.3 11.6 %collective-permute-start.2 = (bf16[1,64,768]{2,1,0:T(8,128)(2,1)}, bf16[1,64,768]{2,1,0:T(8,128)(2,1)S(1)}, u32[]{:S(2)}, u32[]{:S(2)}) collective-permute-start(bf16[1,64,768]{2,1,0:T(8,128)(2,1)} %bitcast.293), channel_id=1, source_target_pairs={{0,24},{4,28},{8,0},{12,4},{16,8},{20,12},{24,16},{28,20},{1,25},{... | collective-permute-start | bytes 294920 | tf_op jit(solution)/shard_map/ppermute | solution.py:676
  33.4 17.3 %collective-permute-start.3 = (bf16[4,64,768]{2,1,0:T(8,128)(2,1)}, bf16[4,64,768]{2,1,0:T(8,128)(2,1)S(1)}, u32[]{:S(2)}, u32[]{:S(2)}) collective-permute-start(bf16[4,64,768]{2,1,0:T(8,128)(2,1)} %join.4.refs_0_), channel_id=1, source_target_pairs={{0,4},{4,0},{8,12},{12,8},{16,20},{20,16},{24,28},{28,24},{1,5},{5... | collective-permute-start | bytes 1179656 | tf_op jit(solution)/shard_map/ppermute | solution.py:676
  34.6 4.9 %collective-permute-start.4 = (bf16[1,144,384]{2,1,0:T(8,128)(2,1)}, bf16[1,144,384]{2,1,0:T(8,128)(2,1)S(1)}, u32[]{:S(2)}, u32[]{:S(2)}) collective-permute-start(bf16[1,144,384]{2,1,0:T(8,128)(2,1)} %bitcast.287), channel_id=1, source_target_pairs={{0,8},{4,12},{8,16},{12,20},{16,24},{20,28},{24,0},{28,4},{1,9},{5... | collective-permute-start | bytes 331784 | tf_op jit(solution)/shard_map/ppermute | solution.py:676
  34.6 5.7 %collective-permute-start.5 = (bf16[1,144,384]{2,1,0:T(8,128)(2,1)}, bf16[1,144,384]{2,1,0:T(8,128)(2,1)S(1)}, u32[]{:S(2)}, u32[]{:S(2)}) collective-permute-start(bf16[1,144,384]{2,1,0:T(8,128)(2,1)} %bitcast.288), channel_id=1, source_target_pairs={{0,16},{4,20},{8,24},{12,28},{16,0},{20,4},{24,8},{28,12},{1,17},{... | collective-permute-start | bytes 331784 | tf_op jit(solution)/shard_map/ppermute | solution.py:676
  35.0 15.7 %collective-permute-start.6 = (bf16[1,144,384]{2,1,0:T(8,128)(2,1)}, bf16[1,144,384]{2,1,0:T(8,128)(2,1)S(1)}, u32[]{:S(2)}, u32[]{:S(2)}) collective-permute-start(bf16[1,144,384]{2,1,0:T(8,128)(2,1)} %bitcast.289), channel_id=1, source_target_pairs={{0,24},{4,28},{8,0},{12,4},{16,8},{20,12},{24,16},{28,20},{1,25},{... | collective-permute-start | bytes 331784 | tf_op jit(solution)/shard_map/ppermute | solution.py:676
  36.1 18.6 %collective-permute-start.7 = (bf16[4,64,768]{2,1,0:T(8,128)(2,1)}, bf16[4,64,768]{2,1,0:T(8,128)(2,1)S(1)}, u32[]{:S(2)}, u32[]{:S(2)}) collective-permute-start(bf16[4,64,768]{2,1,0:T(8,128)(2,1)} %join.4.refs_0_), channel_id=1, source_target_pairs={{0,1},{1,0},{2,3},{3,2},{4,5},{5,4},{6,7},{7,6},{8,9},{9,8},{10,11... | collective-permute-start | bytes 1179656 | tf_op jit(solution)/shard_map/ppermute | solution.py:676
  50.7 4.0 %collective-permute-start.8 = (bf16[4,64,768]{2,1,0:T(8,128)(2,1)S(1)}, bf16[4,64,768]{2,1,0:T(8,128)(2,1)S(1)}, u32[]{:S(2)}, u32[]{:S(2)}) collective-permute-start(bf16[4,64,768]{2,1,0:T(8,128)(2,1)S(1)} %collective-permute-done.3.refs_1_), channel_id=1, source_target_pairs={{0,1},{1,0},{2,3},{3,2},{4,5},{5,4},{6,7},{7,6},{8,9},{9,8},{10,11... | collective-permute-start | bytes 1179656 | tf_op jit(solution)/shard_map/ppermute | solution.py:676
  51.6 12.1 %copy-start.11 = (pred[1023,256]{1,0:T(8,128)(4,1)}, pred[1023,256]{1,0:T(8,128)(4,1)S(1)}, u32[]{:S(2)}) copy-start(pred[1023,256]{1,0:T(8,128)(4,1)S(1)} %iota_compare_fusion) | copy-start | bytes 785668
  53.5 10.2 %collective-permute-start.10 = (bf16[4,96,384]{2,1,0:T(8,128)(2,1)}, bf16[4,96,384]{2,1,0:T(8,128)(2,1)}, u32[]{:S(2)}, u32[]{:S(2)}) collective-permute-start(bf16[4,96,384]{2,1,0:T(8,128)(2,1)} %get-tuple-element.174.refs_0_), channel_id=1, source_target_pairs={{0,2},{1,3},{2,0},{3,1},{4,6},{5,7},{6,4},{7,5},{8,10},{9,11},{10,... | collective-permute-start | bytes 884744 | tf_op jit(solution)/shard_map/ppermute | solution.py:676
  54.7 9.0 %collective-permute-start.9 = (bf16[4,48,384]{2,1,0:T(8,128)(2,1)}, bf16[4,48,384]{2,1,0:T(8,128)(2,1)S(1)}, u32[]{:S(2)}, u32[]{:S(2)}) collective-permute-start(bf16[4,48,384]{2,1,0:T(8,128)(2,1)} %get-tuple-element.168.refs_0_), channel_id=1, source_target_pairs={{0,4},{4,0},{8,12},{12,8},{16,20},{20,16},{24,28},{28,24},{1,5},{5... | collective-permute-start | bytes 442376 | tf_op jit(solution)/shard_map/ppermute | solution.py:676
  65.7 21.1 %copy-start.5 = (bf16[8,96,384]{2,1,0:T(8,128)(2,1)S(1)}, bf16[8,96,384]{2,1,0:T(8,128)(2,1)}, u32[]{:S(2)}) copy-start(bf16[8,96,384]{2,1,0:T(8,128)(2,1)} %join.7.refs_4_) | copy-start | bytes 1769476
  65.7 17.8 %collective-permute-start.12 = (bf16[8,96,384]{2,1,0:T(8,128)(2,1)}, bf16[8,96,384]{2,1,0:T(8,128)(2,1)S(1)}, u32[]{:S(2)}, u32[]{:S(2)}) collective-permute-start(bf16[8,96,384]{2,1,0:T(8,128)(2,1)} %join.7.refs_4_), channel_id=1, source_target_pairs={{0,4},{4,0},{8,12},{12,8},{16,20},{20,16},{24,28},{28,24},{1,5},{5... | collective-permute-start | bytes 1769480 | tf_op jit(solution)/shard_map/ppermute | solution.py:676
  68.8 15.4 %copy-start.9 = (bf16[8,48,384]{2,1,0:T(8,128)(2,1)S(1)}, bf16[8,48,384]{2,1,0:T(8,128)(2,1)}, u32[]{:S(2)}) copy-start(bf16[8,48,384]{2,1,0:T(8,128)(2,1)} %join.6.refs_0_) | copy-start | bytes 884740
  68.8 11.5 %collective-permute-start.11 = (bf16[8,48,384]{2,1,0:T(8,128)(2,1)}, bf16[8,48,384]{2,1,0:T(8,128)(2,1)S(1)}, u32[]{:S(2)}, u32[]{:S(2)}) collective-permute-start(bf16[8,48,384]{2,1,0:T(8,128)(2,1)} %join.6.refs_0_), channel_id=1, source_target_pairs={{0,2},{1,3},{2,0},{3,1},{4,6},{5,7},{6,4},{7,5},{8,10},{9,11},{10,... | collective-permute-start | bytes 884744 | tf_op jit(solution)/shard_map/ppermute | solution.py:676
  69.1 17.2 %collective-permute-start.15 = (bf16[8,96,384]{2,1,0:T(8,128)(2,1)}, bf16[8,96,384]{2,1,0:T(8,128)(2,1)}, u32[]{:S(2)}, u32[]{:S(2)}) collective-permute-start(bf16[8,96,384]{2,1,0:T(8,128)(2,1)} %join.7.refs_4_), channel_id=1, source_target_pairs={{0,1},{1,0},{2,3},{3,2},{4,5},{5,4},{6,7},{7,6},{8,9},{9,8},{10,11... | collective-permute-start | bytes 1769480 | tf_op jit(solution)/shard_map/ppermute | solution.py:676
  83.5 3.3 collective-permute-start.16
  84.3 2.0 collective-permute-start.13
  84.3 2.5 collective-permute-start.14
  185.6 11.4 %collective-permute-start.17 = (bf16[4,4,96,768]{3,2,1,0:T(8,128)(2,1)}, bf16[4,4,96,768]{3,2,1,0:T(8,128)(2,1)}, u32[]{:S(2)}, u32[]{:S(2)}) collective-permute-start(bf16[4,4,96,768]{3,2,1,0:T(8,128)(2,1)} %get-tuple-element.217), channel_id=1, source_target_pairs={{0,1},{1,0},{2,3},{3,2},{4,5},{5,4},{6,7},{7,6},{8,9},{9,8},{10,11... | collective-permute-start | bytes 7077896 | tf_op jit(solution)/shard_map/ppermute | solution.py:676
  198.9 27.4 %collective-permute-start.18 = (bf16[2,4,96,768]{3,2,1,0:T(8,128)(2,1)S(1)}, bf16[2,4,96,768]{3,2,1,0:T(8,128)(2,1)}, u32[]{:S(2)}, u32[]{:S(2)}) collective-permute-start(bf16[2,4,96,768]{3,2,1,0:T(8,128)(2,1)S(1)} %fusion.2), channel_id=1, source_target_pairs={{0,2},{1,3},{2,0},{3,1},{4,6},{5,7},{6,4},{7,5},{8,10},{9,11},{10,... | collective-permute-start | bytes 3538952 | tf_op jit(solution)/shard_map/ppermute | solution.py:676
  226.3 19.3 %collective-permute-start.20 = (bf16[384,3840]{1,0:T(8,128)(2,1)}, bf16[384,3840]{1,0:T(8,128)(2,1)}, u32[]{:S(2)}, u32[]{:S(2)}) collective-permute-start(bf16[384,3840]{1,0:T(8,128)(2,1)} %get-tuple-element.237), channel_id=1, source_target_pairs={{0,1},{1,0},{2,3},{3,2},{4,5},{5,4},{6,7},{7,6},{8,9},{9,8},{10,11... | collective-permute-start | bytes 8847368 | tf_op jit(solution)/shard_map/ppermute | solution.py:676
  229.1 16.5 %collective-permute-start.19 = (bf16[4,96,768]{2,1,0:T(8,128)(2,1)S(1)}, bf16[4,96,768]{2,1,0:T(8,128)(2,1)S(1)}, u32[]{:S(2)}, u32[]{:S(2)}) collective-permute-start(bf16[4,96,768]{2,1,0:T(8,128)(2,1)S(1)} %fusion.3), channel_id=1, source_target_pairs={{0,4},{4,0},{8,12},{12,8},{16,20},{20,16},{24,28},{28,24},{1,5},{5... | collective-permute-start | bytes 1769480 | tf_op jit(solution)/shard_map/ppermute | solution.py:676
  249.1 36.7 %collective-permute-start.26 = (bf16[2,4,24,3840]{3,2,1,0:T(8,128)(2,1)}, bf16[2,4,24,3840]{3,2,1,0:T(8,128)(2,1)}, u32[]{:S(2)}, u32[]{:S(2)}) collective-permute-start(bf16[2,4,24,3840]{3,2,1,0:T(8,128)(2,1)} %fusion), channel_id=1, source_target_pairs={{0,4},{4,0},{8,12},{12,8},{16,20},{20,16},{24,28},{28,24},{1,5},{5... | collective-permute-start | bytes 4423688 | tf_op jit(solution)/shard_map/ppermute | solution.py:676
  249.4 2.2 collective-permute-start.21
  253.2 32.6 %collective-permute-start.22 = (bf16[2,4,24,768]{3,2,1,0:T(8,128)(2,1)}, bf16[2,4,24,768]{3,2,1,0:T(8,128)(2,1)}, u32[]{:S(2)}, u32[]{:S(2)}) collective-permute-start(bf16[2,4,24,768]{3,2,1,0:T(8,128)(2,1)} %fusion.18), channel_id=1, source_target_pairs={{0,2},{1,3},{2,0},{3,1},{4,6},{5,7},{6,4},{7,5},{8,10},{9,11},{10,... | collective-permute-start | bytes 884744 | tf_op jit(solution)/shard_map/ppermute | solution.py:676
  256.7 29.1 %collective-permute-start.23 = (bf16[96,768]{1,0:T(8,128)(2,1)}, bf16[96,768]{1,0:T(8,128)(2,1)}, u32[]{:S(2)}, u32[]{:S(2)}) collective-permute-start(bf16[96,768]{1,0:T(8,128)(2,1)} %get-tuple-element.366), channel_id=1, source_target_pairs={{0,8},{4,12},{8,16},{12,20},{16,24},{20,28},{24,0},{28,4},{1,9},{5... | collective-permute-start | bytes 442376 | tf_op jit(solution)/shard_map/ppermute | solution.py:676
  257.2 28.6 %collective-permute-start.24 = (bf16[96,768]{1,0:T(8,128)(2,1)}, bf16[96,768]{1,0:T(8,128)(2,1)}, u32[]{:S(2)}, u32[]{:S(2)}) collective-permute-start(bf16[96,768]{1,0:T(8,128)(2,1)} %get-tuple-element.365), channel_id=1, source_target_pairs={{0,16},{4,20},{8,24},{12,28},{16,0},{20,4},{24,8},{28,12},{1,17},{... | collective-permute-start | bytes 442376 | tf_op jit(solution)/shard_map/ppermute | solution.py:676
  258.6 27.2 %collective-permute-start.25 = (bf16[96,768]{1,0:T(8,128)(2,1)S(1)}, bf16[96,768]{1,0:T(8,128)(2,1)}, u32[]{:S(2)}, u32[]{:S(2)}) collective-permute-start(bf16[96,768]{1,0:T(8,128)(2,1)S(1)} %get-tuple-element.364), channel_id=1, source_target_pairs={{0,24},{4,28},{8,0},{12,4},{16,8},{20,12},{24,16},{28,20},{1,25},{... | collective-permute-start | bytes 442376 | tf_op jit(solution)/shard_map/ppermute | solution.py:676
  285.8 7.0 %collective-permute-start.27 = (bf16[384,1536]{1,0:T(8,128)(2,1)}, bf16[384,1536]{1,0:T(8,128)(2,1)}, u32[]{:S(2)}, u32[]{:S(2)}) collective-permute-start(bf16[384,1536]{1,0:T(8,128)(2,1)} %get-tuple-element.269), channel_id=1, source_target_pairs={{0,1},{1,0},{2,3},{3,2},{4,5},{5,4},{6,7},{7,6},{8,9},{9,8},{10,11... | collective-permute-start | bytes 3538952 | tf_op jit(solution)/shard_map/ppermute | solution.py:676
  290.1 19.9 %collective-permute-start.31 = (bf16[4,24,3840]{2,1,0:T(8,128)(2,1)}, bf16[4,24,3840]{2,1,0:T(8,128)(2,1)}, u32[]{:S(2)}, u32[]{:S(2)}) collective-permute-start(bf16[4,24,3840]{2,1,0:T(8,128)(2,1)} %fusion.1), channel_id=1, source_target_pairs={{0,2},{1,3},{2,0},{3,1},{4,6},{5,7},{6,4},{7,5},{8,10},{9,11},{10,... | collective-permute-start | bytes 2211848 | tf_op jit(solution)/shard_map/ppermute | solution.py:676
  291.5 18.5 %collective-permute-start.30 = (bf16[4,24,768]{2,1,0:T(8,128)(2,1)S(1)}, bf16[4,24,768]{2,1,0:T(8,128)(2,1)}, u32[]{:S(2)}, u32[]{:S(2)}) collective-permute-start(bf16[4,24,768]{2,1,0:T(8,128)(2,1)S(1)} %fusion.22), channel_id=1, source_target_pairs={{0,4},{4,0},{8,12},{12,8},{16,20},{20,16},{24,28},{28,24},{1,5},{5... | collective-permute-start | bytes 442376 | tf_op jit(solution)/shard_map/ppermute | solution.py:676
  295.8 22.4 %collective-permute-start.32 = (bf16[2,4,24,1536]{3,2,1,0:T(8,128)(2,1)}, bf16[2,4,24,1536]{3,2,1,0:T(8,128)(2,1)}, u32[]{:S(2)}, u32[]{:S(2)}) collective-permute-start(bf16[2,4,24,1536]{3,2,1,0:T(8,128)(2,1)} %fusion.9), channel_id=1, source_target_pairs={{0,4},{4,0},{8,12},{12,8},{16,20},{20,16},{24,28},{28,24},{1,5},{5... | collective-permute-start | bytes 1769480 | tf_op jit(solution)/shard_map/ppermute | solution.py:676
  300.0 4.4 %collective-permute-start.28 = (bf16[16,1536]{1,0:T(8,128)(2,1)S(1)}, bf16[16,1536]{1,0:T(8,128)(2,1)S(1)}, u32[]{:S(2)}, u32[]{:S(2)}) collective-permute-start(bf16[16,1536]{1,0:T(8,128)(2,1)S(1)} %fusion.35), channel_id=1, source_target_pairs={{0,1},{1,0},{2,3},{3,2},{4,5},{5,4},{6,7},{7,6},{8,9},{9,8},{10,11... | collective-permute-start | bytes 147464 | tf_op jit(solution)/shard_map/ppermute | solution.py:676
  304.4 7.0 %collective-permute-start.29 = (bf16[16,1536]{1,0:T(8,128)(2,1)S(1)}, bf16[16,1536]{1,0:T(8,128)(2,1)S(1)}, u32[]{:S(2)}, u32[]{:S(2)}) collective-permute-start(bf16[16,1536]{1,0:T(8,128)(2,1)S(1)} %fusion.60), channel_id=1, source_target_pairs={{0,4},{4,0},{8,12},{12,8},{16,20},{20,16},{24,28},{28,24},{1,5},{5... | collective-permute-start | bytes 147464 | tf_op jit(solution)/shard_map/ppermute | solution.py:676
  314.0 9.4 %collective-permute-start.37 = (bf16[24,3840]{1,0:T(8,128)(2,1)}, bf16[24,3840]{1,0:T(8,128)(2,1)S(1)}, u32[]{:S(2)}, u32[]{:S(2)}) collective-permute-start(bf16[24,3840]{1,0:T(8,128)(2,1)} %get-tuple-element.363), channel_id=1, source_target_pairs={{0,8},{4,12},{8,16},{12,20},{16,24},{20,28},{24,0},{28,4},{1,9},{5... | collective-permute-start | bytes 552968 | tf_op jit(solution)/shard_map/ppermute | solution.py:676
  315.4 15.0 %collective-permute-start.38 = (bf16[24,3840]{1,0:T(8,128)(2,1)S(1)}, bf16[24,3840]{1,0:T(8,128)(2,1)S(1)}, u32[]{:S(2)}, u32[]{:S(2)}) collective-permute-start(bf16[24,3840]{1,0:T(8,128)(2,1)S(1)} %get-tuple-element.362), channel_id=1, source_target_pairs={{0,16},{4,20},{8,24},{12,28},{16,0},{20,4},{24,8},{28,12},{1,17},{... | collective-permute-start | bytes 552968 | tf_op jit(solution)/shard_map/ppermute | solution.py:676
  318.1 15.1 %collective-permute-start.39 = (bf16[24,3840]{1,0:T(8,128)(2,1)S(1)}, bf16[24,3840]{1,0:T(8,128)(2,1)S(1)}, u32[]{:S(2)}, u32[]{:S(2)}) collective-permute-start(bf16[24,3840]{1,0:T(8,128)(2,1)S(1)} %get-tuple-element.361), channel_id=1, source_target_pairs={{0,24},{4,28},{8,0},{12,4},{16,8},{20,12},{24,16},{28,20},{1,25},{... | collective-permute-start | bytes 552968 | tf_op jit(solution)/shard_map/ppermute | solution.py:676
  319.3 13.9 %collective-permute-start.33 = (bf16[112,1536]{1,0:T(8,128)(2,1)S(1)}, bf16[112,1536]{1,0:T(8,128)(2,1)S(1)}, u32[]{:S(2)}, u32[]{:S(2)}) collective-permute-start(bf16[112,1536]{1,0:T(8,128)(2,1)S(1)} %pad_maximum_fusion), channel_id=1, source_target_pairs={{0,2},{1,3},{2,0},{3,1},{4,6},{5,7},{6,4},{7,5},{8,10},{9,11},{10,... | collective-permute-start | bytes 1032200 | tf_op jit(solution)/shard_map/ppermute | solution.py:676
  334.5 4.7 %collective-permute-start.34 = (bf16[40,2304]{1,0:T(8,128)(2,1)S(1)}, bf16[40,2304]{1,0:T(8,128)(2,1)S(1)}, u32[]{:S(2)}, u32[]{:S(2)}) collective-permute-start(bf16[40,2304]{1,0:T(8,128)(2,1)S(1)} %get-tuple-element.378), channel_id=1, source_target_pairs={{0,8},{4,12},{8,16},{12,20},{16,24},{20,28},{24,0},{28,4},{1,9},{5... | collective-permute-start | bytes 552968 | tf_op jit(solution)/shard_map/ppermute | solution.py:676
  334.6 14.5 %collective-permute-start.35 = (bf16[40,2304]{1,0:T(8,128)(2,1)S(1)}, bf16[40,2304]{1,0:T(8,128)(2,1)S(1)}, u32[]{:S(2)}, u32[]{:S(2)}) collective-permute-start(bf16[40,2304]{1,0:T(8,128)(2,1)S(1)} %get-tuple-element.379), channel_id=1, source_target_pairs={{0,16},{4,20},{8,24},{12,28},{16,0},{20,4},{24,8},{28,12},{1,17},{... | collective-permute-start | bytes 552968 | tf_op jit(solution)/shard_map/ppermute | solution.py:676
  335.0 17.0 %collective-permute-start.36 = (bf16[40,2304]{1,0:T(8,128)(2,1)S(1)}, bf16[40,2304]{1,0:T(8,128)(2,1)S(1)}, u32[]{:S(2)}, u32[]{:S(2)}) collective-permute-start(bf16[40,2304]{1,0:T(8,128)(2,1)S(1)} %get-tuple-element.377), channel_id=1, source_target_pairs={{0,24},{4,28},{8,0},{12,4},{16,8},{20,12},{24,16},{28,20},{1,25},{... | collective-permute-start | bytes 552968 | tf_op jit(solution)/shard_map/ppermute | solution.py:676
  336.4 22.2 %copy-start.1 = (bf16[96,3072]{1,0:T(8,128)(2,1)S(1)}, bf16[96,3072]{1,0:T(8,128)(2,1)}, u32[]{:S(2)}) copy-start(bf16[96,3072]{1,0:T(8,128)(2,1)} %param.31) | copy-start | bytes 1769476
  (28 other events, 152.1 us)
Sparse Core Ops, SparseCore 0:
  11.0 73.2 all-gather.2
  87.1 63.8 all-gather.4
